TPU v7x, 256 devices: a whole 4x4x8 slice. The times are simulated.
256 devices in a mesh: tiles: 64 (over y, z, core), rep: 4 (over x).
Axes of the slice: x: 4, y: 4, z: 8, core: 2. Of those that a mesh axis runs over, the one named last changes fastest.
Arguments:
- trailing_tiles: float32 [5120, 256, 256], P(('tiles', 'rep')), may hold values from -6 to 6
- panel_rows: float32 [128, 256, 512], P('tiles'), may hold values from -3 to 3
- pivot_blocks: float32 [2, 256, 256], replicated
- coupling: float32 [256, 256], replicated, may hold values from -0.1875 to 0.1875
- row_ids: int32 [128], replicated, may hold values from 2 to 96, as said below
- membership: int32 [64, 24], replicated, may hold values from 2 to 96, as said below
- tile_pairs: int32 [5120, 2], P(('tiles', 'rep')), may hold values from 0 to 24, as said below
Outputs:
- updated_tiles: float32 [5120, 256, 256], P(('tiles', 'rep'))
- factors: float32 [128, 256, 512], P('tiles')
- pivot_diag: float32 [2, 256], replicated
Inputs may be any that keep to these rules, and one draw needn't show every extreme that they name: `row_ids`: each row block 2 to 95 stands in exactly one slot; the other slots hold 96. `membership`: entries are row blocks 2 to 95, or 96 for none. `tile_pairs`: a slot's first entry is below 12, its second from 12 to 23, or both are 24 for an empty slot; over all devices every unordered pair of row blocks 2 to 96 - 1 (a block with itself too) is listed exactly once; some device fills all 20 slots.
All inputs are finite; a program needn't handle non-finite values.
Results may differ from a plain program's by a relative error of at most 0.00005.
Values sent between devices are 32-bit elements; how exact they have to be, the bound alone decides.
No kernel may reach another device: no remote copies, remote signals or barrier semaphores. Data moves between devices by JAX's collectives and lax.ppermute only.
A program may use at most 128 MiB of HBM per device.

v0:
```python
import functools

import jax
import jax.numpy as jnp
from jax import lax
from jax.experimental import pallas as pl
from jax.experimental.pallas import tpu as pltpu
from jax.sharding import PartitionSpec as P


NB = 96
NY, NZ = 4, 8
SPLIT = 128
W = 64
GROUP = 4
F32 = jnp.float32
BF = jnp.bfloat16
HI = lax.Precision.HIGHEST


def dot(a, b):
    return lax.dot_general(a, b, (((1,), (0,)), ((), ())), precision=HI, preferred_element_type=F32)


def dot_nt(a, b):
    return lax.dot_general(a, b, (((1,), (1,)), ((), ())), precision=HI, preferred_element_type=F32)


def split(x):
    hi = x.astype(BF)
    return hi, (x - hi.astype(F32)).astype(BF)


def dot3(ah, al, bh, bl, nt=False):
    dims = (((1,), (1 if nt else 0,)), ((), ()))
    f = functools.partial(lax.dot_general, dimension_numbers=dims, preferred_element_type=F32)
    return f(ah, bh) + (f(ah, bl) + f(al, bh))


def load_panel(state, work, at):
    lo, up = at * W, (at + 1) * W
    eye = lax.broadcasted_iota(jnp.int32, (W, W), 0) == lax.broadcasted_iota(jnp.int32, (W, W), 1)
    work[...] = jnp.concatenate([state[lo:up, lo:up], eye.astype(F32)], axis=1)


def pivot_steps(work):
    rows = lax.broadcasted_iota(jnp.int32, (W, 2 * W), 0)
    aug = work[...]
    for first in range(0, W, GROUP):
        columns = [jnp.broadcast_to(aug[:, k : k + 1], (W, 2 * W)) for k in range(first, first + GROUP)]
        for k in range(first, first + GROUP):
            column = columns[k - first]
            reciprocal = 1.0 / column[k : k + 1, :]
            below = jnp.where(rows > k, column, 0.0)
            aug = aug - below * (aug[k : k + 1, :] * reciprocal)
            for later in range(k + 1 - first, GROUP):
                columns[later] = columns[later] - below * (columns[later][k : k + 1, :] * reciprocal)
    work[...] = aug


def finish_panel(state, work, diag, at, n):
    lo, up = at * W, (at + 1) * W
    rows = lax.broadcasted_iota(jnp.int32, (W, 2 * W), 0)
    lanes = lax.broadcasted_iota(jnp.int32, (W, 2 * W), 1)
    aug = work[...]
    inverse = aug[:, W:]
    on_diag = jnp.where(rows == lanes, aug, 0.0)
    d_col = jnp.sum(on_diag, axis=1, keepdims=True)
    diag[0:1, (at % 2) * W : (at % 2 + 1) * W] = jnp.sum(on_diag, axis=0, keepdims=True)[:, :W]
    width = state.shape[1]
    col = lax.broadcasted_iota(jnp.int32, (W, width), 1)
    row = lax.broadcasted_iota(jnp.int32, (W, width), 0)
    own = jnp.where((col >= lo) & (col < up), (col - lo == row).astype(F32), state[lo:up, :])
    if up < n:
        below = dot(dot_nt(state[up:n, lo:up], inverse), inverse / d_col)
        base = state[up:n, :]
        bcol = lax.broadcasted_iota(jnp.int32, base.shape, 1)
        base = jnp.where((bcol >= lo) & (bcol < up), 0.0, base)
        state[up:n, :] = base - dot(below, own)
    state[lo:up, :] = jnp.where(col < up, dot(inverse, own), 0.0)


def eliminate(state, diag, work, at):
    @pl.loop(0, 2)
    def _(i):
        for p in range(2):

            @pl.when(i == p)
            def _():
                load_panel(state, work, at + p)

        pivot_steps(work)
        for p in range(2):

            @pl.when(i == p)
            def _():
                finish_panel(state, work, diag, at + p, state.shape[0])


def first_kernel(pivot, coupling, state, diag, work):
    h = coupling.shape[0]
    state[:h, :h] = pivot[0]
    state[h:, :h] = coupling[...]
    state[:h, h:] = coupling[...].T
    state[h:, h:] = pivot[1]
    eliminate(state, diag, work, 0)


def middle_kernel(at, before, state, diag, work):
    state[...] = before[...]
    eliminate(state, diag, work, at)


def last_kernel(at, before, d0, d1, d2, high, low, full_high, full_low, diag, state, last, scaled, work):
    state[...] = before[...]
    eliminate(state, last, work, at)
    for p, d in enumerate((d0, d1, d2, last)):
        diag[0:1, p * 2 * W : (p + 1) * 2 * W] = d[...]
    turned = state[...].T
    high[...], low[...] = split(turned)
    scaled[...] = turned / diag[...]
    step = 2 * W

    @pl.loop(0, state.shape[0] // step)
    def _(i):
        at = pl.ds(pl.multiple_of(i * step, step), step)
        full_high[at, :], full_low[at, :] = split(dot(scaled[at, :], state[...]))


def cost(flops, nbytes):
    return pl.CostEstimate(flops=int(flops), bytes_accessed=int(nbytes), transcendentals=0)


def factorize(pivot_blocks, coupling):
    n = 2 * coupling.shape[0]
    full = jax.ShapeDtypeStruct((n, n), F32)
    half = jax.ShapeDtypeStruct((n, n), BF)
    dshape = jax.ShapeDtypeStruct((1, 2 * W), F32)
    work = cost(6e9, 2 * n * n * 4)
    diags = []
    panel = pltpu.VMEM((W, 2 * W), F32)
    state, d = pl.pallas_call(
        first_kernel, out_shape=(full, dshape), scratch_shapes=[panel], cost_estimate=work, name="panels0"
    )(pivot_blocks, coupling)
    diags.append(d)
    for at in (2, 4):
        state, d = pl.pallas_call(
            functools.partial(middle_kernel, at), out_shape=(full, dshape), scratch_shapes=[panel], cost_estimate=work
        )(state)
        diags.append(d)
    return pl.pallas_call(
        functools.partial(last_kernel, 6),
        out_shape=(half, half, half, half, jax.ShapeDtypeStruct((1, n), F32)),
        scratch_shapes=[pltpu.VMEM((n, n), F32), pltpu.VMEM((1, 2 * W), F32), pltpu.VMEM((n, n), F32), panel],
        cost_estimate=work,
        name="panels6",
    )(state, *diags)


def apply_inverse(x, high, low):
    h = high.shape[0] // 2
    xh, xl = split(x)
    first = dot3(xh[:, :h], xl[:, :h], high[:h, :h], low[:h, :h])
    second = dot3(xh, xl, high[:, h:], low[:, h:])
    return jnp.concatenate([first, second], axis=1)


def own_kernel(keep, x, high, low, diag, out):
    i = pl.program_id(0)
    y = apply_inverse(x[0], high, low) / diag[...]
    out[0] = jnp.where(keep[i] > 0, y, 0.0)


def own_factors(panel_rows, high, low, diag, usable):
    slots, b, n = panel_rows.shape
    const = lambda i, k: (0, 0)
    return pl.pallas_call(
        own_kernel,
        out_shape=jax.ShapeDtypeStruct(panel_rows.shape, F32),
        grid_spec=pltpu.PrefetchScalarGridSpec(
            num_scalar_prefetch=1,
            grid=(slots,),
            in_specs=[
                pl.BlockSpec((1, b, n), lambda i, k: (i, 0, 0)),
                pl.BlockSpec((n, n), const),
                pl.BlockSpec((n, n), const),
                pl.BlockSpec((1, n), const),
            ],
            out_specs=pl.BlockSpec((1, b, n), lambda i, k: (i, 0, 0)),
        ),
        cost_estimate=cost(slots * b * n * n * 6, slots * b * n * 8),
        name="own_factors",
    )(usable.astype(jnp.int32), panel_rows, high, low, diag)


def pick_kernel(place, *refs):
    nz, ny = 8, 4
    zy = refs[:nz]
    yz = refs[nz : nz + ny]
    outs = refs[nz + ny : nz + ny + 2]
    sems = refs[nz + ny + 2]
    count, rows, _ = outs[0].shape
    half = rows // 2

    def copy(color, which, g, source, at):
        target = outs[which].at[g, pl.ds(color * half, half)]
        return pltpu.make_async_copy(source.at[at], target, sems.at[color, which, g])

    for which in range(2):

        @pl.loop(0, count)
        def _(g):
            ez, ey, slot = place[which, 0, g], place[which, 1, g], place[which, 2, g]
            for e in range(nz):

                @pl.when(ez == e)
                def _():
                    copy(0, which, g, zy[e], ey * 2 + slot).start()

            for e in range(ny):

                @pl.when(ey == e)
                def _():
                    copy(1, which, g, yz[e], ez * 2 + slot).start()

    for which in range(2):

        @pl.loop(0, count)
        def _(g):
            copy(0, which, g, zy[0], 0).wait()
            copy(1, which, g, yz[0], 0).wait()


def pick(zy, yz, place, rows, n):
    count = place.shape[2]
    shape = jax.ShapeDtypeStruct((count, rows, n), F32)
    return pl.pallas_call(
        pick_kernel,
        out_shape=(shape, shape),
        grid_spec=pltpu.PrefetchScalarGridSpec(
            num_scalar_prefetch=1,
            grid=(),
            in_specs=[pl.BlockSpec(memory_space=pl.ANY)] * (len(zy) + len(yz)),
            out_specs=(pl.BlockSpec(memory_space=pltpu.VMEM),) * 2,
            scratch_shapes=[pltpu.SemaphoreType.DMA((2, 2, count))],
        ),
        cost_estimate=cost(0, 4 * 4 * count * rows * n),
        name="pick",
    )(place, *zy, *yz)


def update_kernel(info, tile, full_high, full_low, p0, p1, p2, p3, table, out, stage, lh, ll, rh, rl, sems):
    k = pl.program_id(0)
    count, b, _ = stage.shape
    half = count // 2
    rows = p0.shape[1]
    tail = table.shape[1]

    @pl.when(k == 0)
    def _():
        parts = [
            pltpu.make_async_copy(p, stage.at[:, pl.ds(pl.multiple_of(info[3, i] * rows, rows), rows), :], sems.at[count + i])
            for i, p in enumerate((p0, p1, p2, p3))
        ]
        for c in parts:
            c.start()

        def rest(g):
            return pltpu.make_async_copy(table.at[info[4, g]], stage.at[g, pl.ds(b - tail, tail), :], sems.at[g])

        @pl.loop(0, count)
        def _(g):
            rest(g).start()

        for c in parts:
            c.wait()

        @pl.loop(0, half)
        def _(g):
            rest(g).wait()
            x = jnp.where(info[5, g] > 0, stage[g], 0.0)
            xh, xl = split(x)
            yh, yl = split(dot3(xh, xl, full_high[...], full_low[...]))
            lh[g] = yh
            ll[g] = yl

        @pl.loop(half, count)
        def _(g):
            rest(g).wait()
            x = jnp.where(info[5, g] > 0, stage[g], 0.0)
            xh, xl = split(x)
            rh[g - half] = xh
            rl[g - half] = xl

    @pl.loop(0, tile.shape[0])
    def _(t):
        slot = k * tile.shape[0] + t
        live = info[2, slot] > 0

        @pl.when(live)
        def _():
            i, j = info[0, slot], info[1, slot]
            out[t] = tile[t] - dot3(lh[i], ll[i], rh[j], rl[j], nt=True)

        @pl.when(jnp.logical_not(live))
        def _():
            out[t] = tile[t]


def update_tiles(tiles, full_high, full_low, parts, quarters, table, slots, valid, pairs):
    total, b, _ = tiles.shape
    count = slots.shape[0]
    half = count // 2
    n = full_high.shape[0]
    widest = max(total, count)
    fit = lambda v: jnp.pad(v.astype(jnp.int32), (0, widest - v.shape[0]))
    info = jnp.stack(
        [
            fit(jnp.minimum(pairs[:, 0], half - 1)),
            fit(jnp.clip(pairs[:, 1] - half, 0, half - 1)),
            fit(pairs[:, 0] < count),
            fit(jnp.stack(quarters)),
            fit(slots),
            fit(valid),
        ]
    )
    block = 4 if total % 4 == 0 else 1
    tspec = pl.BlockSpec((block, b, b), lambda k, s: (k, 0, 0))
    whole = pl.BlockSpec((n, n), lambda k, s: (0, 0))
    anywhere = pl.BlockSpec(memory_space=pl.ANY)
    operand = pltpu.VMEM((half, b, n), BF)
    return pl.pallas_call(
        update_kernel,
        out_shape=jax.ShapeDtypeStruct(tiles.shape, F32),
        grid_spec=pltpu.PrefetchScalarGridSpec(
            num_scalar_prefetch=1,
            grid=(total // block,),
            in_specs=[tspec, whole, whole] + [anywhere] * 5,
            out_specs=tspec,
            scratch_shapes=[pltpu.VMEM((count, b, n), F32)]
            + [operand] * 4
            + [pltpu.SemaphoreType.DMA((count + 4,))],
        ),
        compiler_params=pltpu.CompilerParams(vmem_limit_bytes=58 * 2**20),
        cost_estimate=cost(total * b * b * n * 6 + half * b * n * n * 6, total * b * 8 * b + count * b * n * 4),
        name="update_tiles",
    )(info, tiles, full_high, full_low, *parts, table)


def turned(core, step):
    return step if core == 0 else -step


def tile_of(y, z, core):
    return ((y % NY) * NZ + z % NZ) * 2 + core


def chips():
    return [(y, z, c) for y in range(NY) for z in range(NZ) for c in range(2)]


def z_perm(step):
    return [(tile_of(y, z, c), tile_of(y, z + turned(c, step), c)) for y, z, c in chips()]


def y_perm(step):
    return [(tile_of(y, z, c), tile_of(y + turned(c, step), z, c)) for y, z, c in chips()]


def x_perm(tiles, reps, step):
    return [(t * reps + x, t * reps + (x + turned(t % 2, step)) % reps) for t in range(tiles) for x in range(reps)]


def ring(block, size, ahead, back):
    near, far = [block], [block]
    for k in range(size // 2):
        near.append(lax.ppermute(near[-1], "tiles", ahead))
        if k < size // 2 - 1:
            far.append(lax.ppermute(far[-1], "tiles", back))
    return near + far[:0:-1]


def per_device(tiles, reps, trailing_tiles, panel_rows, pivot_blocks, coupling, row_ids, membership, tile_pairs):
    owned_slots, b, n = panel_rows.shape
    tile_index = lax.axis_index("tiles")
    rep_index = lax.axis_index("rep")
    core, my_z, my_y = tile_index % 2, (tile_index // 2) % NZ, tile_index // (2 * NZ)
    turn = 1 - 2 * core
    own_ids = lax.dynamic_slice_in_dim(row_ids, tile_index * owned_slots, owned_slots)

    quarter = SPLIT // reps
    gathered = lax.all_gather(panel_rows[:, SPLIT:], "tiles", axis=0, tiled=True)
    half = quarter // 2
    top = lax.dynamic_slice_in_dim(panel_rows, rep_index * quarter, half, 1)
    low_rows = lax.dynamic_slice_in_dim(panel_rows, rep_index * quarter + half, half, 1)
    za, zb, ya, yb = z_perm(1), z_perm(-1), y_perm(1), y_perm(-1)
    zy = ring(jnp.concatenate(ring(top, NY, ya, yb), axis=0), NZ, za, zb)
    yz = ring(jnp.concatenate(ring(low_rows, NZ, za, zb), axis=0), NY, ya, yb)

    both_lists = lax.dynamic_slice_in_dim(membership, (tile_index // 2) * 2, 2, 0)
    match = both_lists[:, :, None] == row_ids[None, None, :]
    position = jnp.arange(row_ids.shape[0], dtype=jnp.int32)
    where = jnp.max(jnp.where(match, position[None, None, :], 0), axis=2)
    where = jnp.where(core == 0, where, where[::-1])
    slots = where[0]
    valid = (lax.dynamic_index_in_dim(membership, tile_index, 0, keepdims=False) < NB).astype(jnp.int32)
    ez = (turn * (my_z - (where // 4) % NZ)) % NZ
    ey = (turn * (my_y - where // (4 * NZ))) % NY
    place = jnp.stack([ez, ey, where % owned_slots], axis=1)
    here = (slots // 2) % 2 == core

    mine, theirs = pick(zy, yz, place, quarter, n)
    swap = [(t, t ^ 1) for t in range(tiles)]
    mine = jnp.where(here[:, None, None], mine, lax.ppermute(theirs, "tiles", swap))
    both = ("tiles", "rep")
    ahead, back = x_perm(tiles, reps, 1), x_perm(tiles, reps, -1)
    one = lax.ppermute(mine, both, ahead)
    other = lax.ppermute(mine, both, back)
    far = lax.ppermute(one, both, ahead)
    quarters = [(rep_index + shift + reps) % reps for shift in (0, -turn, turn, 2)]

    high, low, full_high, full_low, diag = factorize(pivot_blocks, coupling)
    factors = own_factors(panel_rows, high, low, diag, own_ids < NB)
    parts = (mine, one, other, far)
    updated = update_tiles(trailing_tiles, full_high, full_low, parts, quarters, gathered, slots, valid, tile_pairs)
    return (updated, factors, diag.reshape(2, b))


def solution(mesh):
    return jax.shard_map(
        functools.partial(per_device, mesh.shape["tiles"], mesh.shape["rep"]),
        mesh=mesh,
        in_specs=(
            P(("tiles", "rep"), None, None),
            P("tiles", None, None),
            P(),
            P(),
            P(),
            P(),
            P(("tiles", "rep"), None),
        ),
        out_specs=(P(("tiles", "rep"), None, None), P("tiles", None, None), P()),
        check_vma=False,
    )
```

profile of v0, /device:TPU:1, one launch (start us, length us, event | category | flops | bytes accessed | tf_op | source)
XLA Modules:
  0.0 197.1 jit_solution(11951760156050541992)
XLA Ops:
  7.2 0.0 copy-start
  7.2 0.0 all-gather.2.cloned.1.call-start
  7.2 1.9 slice.16
  9.1 0.0 all-gather.2.cloned.1.call-update
  9.1 0.9 constant_dynamic-update-slice_fusion.7
  10.0 2.5 %collective-permute-start.14 = (f32[2,16,512]{2,1,0:T(8,128)S(1)}, f32[2,16,512]{2,1,0:T(8,128)S(1)}, u32[]{:S(2)}, u32[]{:S(2)}) collective-permute-start(f32[2,16,512]{2,1,0:T(8,128)S(1)} %get-tuple-element.30), channel_id=1, source_target_pairs={{0,56},{4,12},{8,0},{12,20},{16,8},{20,28},{24,16},{28,36},{32,24}... | collective-permute-start | bytes 196616 | tf_op jit(solution)/shard_map/ppermute | solution.py:379
  12.6 4.0 %collective-permute-start.10 = (f32[2,16,512]{2,1,0:T(8,128)S(1)}, f32[2,16,512]{2,1,0:T(8,128)S(1)}, u32[]{:S(2)}, u32[]{:S(2)}) collective-permute-start(f32[2,16,512]{2,1,0:T(8,128)S(1)} %get-tuple-element.30), channel_id=1, source_target_pairs={{0,8},{4,60},{8,16},{12,4},{16,24},{20,12},{24,32},{28,20},{32,40}... | collective-permute-start | bytes 196616 | tf_op jit(solution)/shard_map/ppermute | solution.py:377
  16.6 2.7 %collective-permute-start = (f32[2,16,512]{2,1,0:T(8,128)S(1)}, f32[2,16,512]{2,1,0:T(8,128)S(1)}, u32[]{:S(2)}, u32[]{:S(2)}) collective-permute-start(f32[2,16,512]{2,1,0:T(8,128)S(1)} %get-tuple-element.33), channel_id=1, source_target_pairs={{0,64},{4,196},{8,72},{12,204},{16,80},{20,212},{24,88},{28,220},{... | collective-permute-start | bytes 196616 | tf_op jit(solution)/shard_map/ppermute | solution.py:377
  19.3 0.0 collective-permute-start.2
  19.3 0.0 collective-permute-done.14
  19.3 0.0 collective-permute-start.15
  19.4 2.7 %collective-permute-start.11 = (f32[2,16,512]{2,1,0:T(8,128)S(1)}, f32[2,16,512]{2,1,0:T(8,128)S(1)}, u32[]{:S(2)}, u32[]{:S(2)}) collective-permute-start(f32[2,16,512]{2,1,0:T(8,128)S(1)} %collective-permute-done.10), channel_id=1, source_target_pairs={{0,8},{4,60},{8,16},{12,4},{16,24},{20,12},{24,32},{28,20},{32,40}... | collective-permute-start | bytes 196616 | tf_op jit(solution)/shard_map/ppermute | solution.py:377
  22.0 2.7 %collective-permute-start.1 = (f32[2,16,512]{2,1,0:T(8,128)S(1)}, f32[2,16,512]{2,1,0:T(8,128)S(1)}, u32[]{:S(2)}, u32[]{:S(2)}) collective-permute-start(f32[2,16,512]{2,1,0:T(8,128)S(1)} %collective-permute-done), channel_id=1, source_target_pairs={{0,64},{4,196},{8,72},{12,204},{16,80},{20,212},{24,88},{28,220},{... | collective-permute-start | bytes 196616 | tf_op jit(solution)/shard_map/ppermute | solution.py:377
  24.7 1.3 collective-permute-done.1
  26.1 0.4 collective-permute-start.3
  26.5 0.0 collective-permute-done.15
  26.5 1.1 collective-permute-start.16
  27.6 1.5 collective-permute-start.12
  29.2 7.2 %collective-permute-done.12 = f32[2,16,512]{2,1,0:T(8,128)S(1)} collective-permute-done((f32[2,16,512]{2,1,0:T(8,128)S(1)}, f32[2,16,512]{2,1,0:T(8,128)S(1)}, u32[]{:S(2)}, u32[]{:S(2)}) %collective-permute-start.12) | collective-permute-done | bytes 65568 | tf_op jit(solution)/shard_map/ppermute | solution.py:377
  36.4 0.4 collective-permute-start.13
  36.8 3.9 %collective-permute-done.13 = f32[2,16,512]{2,1,0:T(8,128)S(1)} collective-permute-done((f32[2,16,512]{2,1,0:T(8,128)S(1)}, f32[2,16,512]{2,1,0:T(8,128)S(1)}, u32[]{:S(2)}, u32[]{:S(2)}) %collective-permute-start.13) | collective-permute-done | bytes 65568 | tf_op jit(solution)/shard_map/ppermute | solution.py:377
  40.8 0.0 collective-permute-done.16
  40.8 0.0 copy-start.4
  40.8 4.3 %collective-permute-start.17 = (f32[16,16,512]{2,1,0:T(8,128)S(1)}, f32[16,16,512]{2,1,0:T(8,128)S(1)}, u32[]{:S(2)}, u32[]{:S(2)}) collective-permute-start(f32[16,16,512]{2,1,0:T(8,128)S(1)} %constant_dynamic-update-slice_fusion.refs_8_), channel_id=1, source_target_pairs={{0,64},{4,196},{8,72},{12,204},{16,80},{20,212},{24,88},{28,220},{... | collective-permute-start | bytes 1572872 | tf_op jit(solution)/shard_map/ppermute | solution.py:377
  45.1 0.0 collective-permute-start.7
  45.1 2.7 %collective-permute-start.4 = (f32[8,16,512]{2,1,0:T(8,128)S(1)}, f32[8,16,512]{2,1,0:T(8,128)S(1)}, u32[]{:S(2)}, u32[]{:S(2)}) collective-permute-start(f32[8,16,512]{2,1,0:T(8,128)S(1)} %collective-permute-done.3.refs_1_), channel_id=1, source_target_pairs={{0,8},{4,60},{8,16},{12,4},{16,24},{20,12},{24,32},{28,20},{32,40}... | collective-permute-start | bytes 786440 | tf_op jit(solution)/shard_map/ppermute | solution.py:377
  47.8 0.1 constant_dynamic-slice_fusion.3
  47.8 0.1 copy.20
  47.9 9.5 %collective-permute-done.7.refs_7_ = f32[8,16,512]{2,1,0:T(8,128)S(1)} collective-permute-done((f32[8,16,512]{2,1,0:T(8,128)S(1)}, f32[8,16,512]{2,1,0:T(8,128)S(1)}, u32[]{:S(2)}, u32[]{:S(2)}) %collective-permute-start.7) | collective-permute-done | bytes 262176 | tf_op jit(solution)/shard_map/ppermute | solution.py:379
  57.4 0.0 collective-permute-start.8
  57.5 2.7 %collective-permute-start.5 = (f32[8,16,512]{2,1,0:T(8,128)S(1)}, f32[8,16,512]{2,1,0:T(8,128)}, u32[]{:S(2)}, u32[]{:S(2)}) collective-permute-start(f32[8,16,512]{2,1,0:T(8,128)S(1)} %collective-permute-done.4.refs_2_), channel_id=1, source_target_pairs={{0,8},{4,60},{8,16},{12,4},{16,24},{20,12},{24,32},{28,20},{32,40}... | collective-permute-start | bytes 786440 | tf_op jit(solution)/shard_map/ppermute | solution.py:377
  60.1 0.2 select_reduce_fusion
  60.4 0.1 collective-permute-start.19
  60.5 2.6 %collective-permute-start.18 = (f32[16,16,512]{2,1,0:T(8,128)S(1)}, f32[16,16,512]{2,1,0:T(8,128)S(1)}, u32[]{:S(2)}, u32[]{:S(2)}) collective-permute-start(f32[16,16,512]{2,1,0:T(8,128)S(1)} %collective-permute-done.17.refs_9_), channel_id=1, source_target_pairs={{0,64},{4,196},{8,72},{12,204},{16,80},{20,212},{24,88},{28,220},{... | collective-permute-start | bytes 1572872 | tf_op jit(solution)/shard_map/ppermute | solution.py:377
  63.2 1.8 collective-permute-done.8.refs_6_
  65.0 0.5 collective-permute-start.9
  65.5 2.1 %collective-permute-start.6 = (f32[8,16,512]{2,1,0:T(8,128)}, f32[8,16,512]{2,1,0:T(8,128)S(1)}, u32[]{:S(2)}, u32[]{:S(2)}) collective-permute-start(f32[8,16,512]{2,1,0:T(8,128)} %collective-permute-done.5.refs_3_), channel_id=1, source_target_pairs={{0,8},{4,60},{8,16},{12,4},{16,24},{20,12},{24,32},{28,20},{32,40}... | collective-permute-start | bytes 786440 | tf_op jit(solution)/shard_map/ppermute | solution.py:377
  67.7 0.6 pad_add_fusion.place
  68.3 1.8 collective-permute-done.19.refs_11_
  70.1 4.4 %collective-permute-done.9.refs_5_ = f32[8,16,512]{2,1,0:T(8,128)S(1)} collective-permute-done((f32[8,16,512]{2,1,0:T(8,128)S(1)}, f32[8,16,512]{2,1,0:T(8,128)S(1)}, u32[]{:S(2)}, u32[]{:S(2)}) %collective-permute-start.9) | collective-permute-done | bytes 262176 | tf_op jit(solution)/shard_map/ppermute | solution.py:379
  74.5 0.7 copy-done.12
  75.2 0.7 copy-done.13
  76.0 0.8 copy-done.7
  76.8 5.4 %pick.1 = (f32[24,32,512]{2,1,0:T(8,128)}, f32[24,32,512]{2,1,0:T(8,128)}) custom-call(s32[2,3,24]{2,1,0:T(4,128)} %pad_add_fusion.place, f32[8,16,512]{2,1,0:T(8,128)} %copy-done.3, f32[8,16,512]{2,1,0:T(8,128)} %copy-done.8, f32[8,16,512]{2,1,0:T(8,128)} %copy-done.10, f32[8,16,512]{2,1,0:T(8,128)} %collective-permute-done.5.refs_3_, ...), custom_call_target="tpu_custom_call" | custom-call | bytes 6291456 | tf_op jit(solution)/shard_map/pick/pallas_call | solution.py:237
  82.2 13.4 %collective-permute-start.20 = (f32[24,32,512]{2,1,0:T(8,128)}, f32[24,32,512]{2,1,0:T(8,128)S(1)}, u32[]{:S(2)}, u32[]{:S(2)}) collective-permute-start(f32[24,32,512]{2,1,0:T(8,128)} %get-tuple-element.25), channel_id=1, source_target_pairs={{0,4},{4,0},{8,12},{12,8},{16,20},{20,16},{24,28},{28,24},{32,36},... | collective-permute-start | bytes 4718600 | tf_op jit(solution)/shard_map/ppermute | solution.py:414
  95.7 4.0 %collective-permute-done.20 = f32[24,32,512]{2,1,0:T(8,128)S(1)} collective-permute-done((f32[24,32,512]{2,1,0:T(8,128)}, f32[24,32,512]{2,1,0:T(8,128)S(1)}, u32[]{:S(2)}, u32[]{:S(2)}) %collective-permute-start.20) | collective-permute-done | bytes 1572896 | tf_op jit(solution)/shard_map/ppermute | solution.py:414
  99.6 1.7 broadcast_select_fusion.p0
  101.3 3.0 %collective-permute-start.21 = (f32[24,32,512]{2,1,0:T(8,128)S(1)}, f32[24,32,512]{2,1,0:T(8,128)S(1)}, u32[]{:S(2)}, u32[]{:S(2)}) collective-permute-start(f32[24,32,512]{2,1,0:T(8,128)S(1)} %broadcast_select_fusion.p0), channel_id=1, source_target_pairs={{0,1},{1,2},{2,3},{3,0},{4,7},{5,4},{6,5},{7,6},{8,9},{9,10},{10,1... | collective-permute-start | bytes 4718600 | tf_op jit(solution)/shard_map/ppermute | solution.py:417
  104.3 10.1 %panels0.1 = (f32[512,512]{1,0:T(8,128)}, f32[1,128]{1,0:T(1,128)}) custom-call(f32[2,256,256]{2,1,0:T(8,128)} %pivot.1, f32[256,256]{1,0:T(8,128)} %coupling.1), custom_call_target="tpu_custom_call" | custom-call | flops 6000000000 | bytes 2097152 | tf_op jit(solution)/shard_map/panels0/pallas_call | solution.py:142
  114.4 9.4 %shard_map.94 = (f32[512,512]{1,0:T(8,128)}, f32[1,128]{1,0:T(1,128)}) custom-call(f32[512,512]{1,0:T(8,128)} %get-tuple-element.16.before), custom_call_target="tpu_custom_call" | custom-call | flops 6000000000 | bytes 2097152 | tf_op jit(solution)/shard_map/pallas_call | solution.py:147
  123.8 8.7 %shard_map.95 = (f32[512,512]{1,0:T(8,128)}, f32[1,128]{1,0:T(1,128)}) custom-call(f32[512,512]{1,0:T(8,128)} %get-tuple-element.17.before), custom_call_target="tpu_custom_call" | custom-call | flops 6000000000 | bytes 2097152 | tf_op jit(solution)/shard_map/pallas_call | solution.py:147
  132.5 2.7 %collective-permute-start.23 = (f32[24,32,512]{2,1,0:T(8,128)S(1)}, f32[24,32,512]{2,1,0:T(8,128)}, u32[]{:S(2)}, u32[]{:S(2)}) collective-permute-start(f32[24,32,512]{2,1,0:T(8,128)S(1)} %collective-permute-done.21.p1), channel_id=1, source_target_pairs={{0,1},{1,2},{2,3},{3,0},{4,7},{5,4},{6,5},{7,6},{8,9},{9,10},{10,1... | collective-permute-start | bytes 4718600 | tf_op jit(solution)/shard_map/ppermute | solution.py:419
  135.2 10.7 %panels6.1 = (bf16[512,512]{1,0:T(8,128)(2,1)}, bf16[512,512]{1,0:T(8,128)(2,1)}, bf16[512,512]{1,0:T(8,128)(2,1)}, bf16[512,512]{1,0:T(8,128)(2,1)}, f32[1,512]{1,0:T(1,128)}) custom-call(f32[512,512]{1,0:T(8,128)} %get-tuple-element.18.before, f32[1,128]{1,0:T(1,128)} %get-tuple-element.19.d0, f32[1,128]{1,0:T(1,128)} %get-tuple-element.20.d1, ...), custom_call_target="tpu_custom_call" | custom-call | flops 6000000000 | bytes 2097152 | tf_op jit(solution)/shard_map/panels6/pallas_call | solution.py:151
  145.9 0.1 constant_dynamic-slice_fusion.2
  146.0 0.1 copy.25
  146.1 0.5 broadcast.169
  146.6 1.3 reduce.3
  147.9 0.6 reshape.62
  148.6 0.1 pad_add_fusion.1
  148.6 0.6 stack.57.info
  149.3 0.6 compare_convert_fusion.keep
  149.9 3.8 %own_factors.1 = f32[2,256,512]{2,1,0:T(8,128)} custom-call(s32[2]{0:T(128)} %compare_convert_fusion.keep, f32[2,256,512]{2,1,0:T(8,128)} %x.9, bf16[512,512]{1,0:T(8,128)(2,1)} %get-tuple-element.26.high, bf16[512,512]{1,0:T(8,128)(2,1)} %get-tuple-element.27.low, f32[1,512]{1,0:T(1,128)} %get-tuple-element.28.diag), custom_call_target="tpu_custom_call" | custom-call | flops 805306368 | bytes 2097152 | tf_op jit(solution)/shard_map/own_factors/pallas_call | solution.py:177
  153.7 14.9 %collective-permute-done.22.p2 = f32[24,32,512]{2,1,0:T(8,128)} collective-permute-done((f32[24,32,512]{2,1,0:T(8,128)S(1)}, f32[24,32,512]{2,1,0:T(8,128)}, u32[]{:S(2)}, u32[]{:S(2)}) %collective-permute-start.22) | collective-permute-done | bytes 1572896 | tf_op jit(solution)/shard_map/ppermute | solution.py:418
  168.6 21.7 %update_tiles.1 = f32[20,256,256]{2,1,0:T(8,128)} custom-call(s32[6,24]{1,0:T(8,128)} %stack.57.info, f32[20,256,256]{2,1,0:T(8,128)} %tile.1, bf16[512,512]{1,0:T(8,128)(2,1)} %get-tuple-element.22.full_high, bf16[512,512]{1,0:T(8,128)(2,1)} %get-tuple-element.23.full_low, f32[24,32,512]{2,1,0:T(8,128)} %copy-done.1, f32[24,32,512]{2,1,0:T(8,128)} %copy-done.2, ...), custom_call_target="tpu_custom_call" | custom-call | flops 8858370048 | bytes 23068672 | tf_op jit(solution)/shard_map/update_tiles/pallas_call | solution.py:332
  (60 shorter events, 0.3 us)
Async XLA Ops:
  7.2 40.6 %copy-start = (s32[64,24]{0,1:T(8,128)S(1)}, s32[64,24]{0,1:T(8,128)}, u32[]{:S(2)}) copy-start(s32[64,24]{0,1:T(8,128)} %param.12) | copy-start | bytes 18436
  7.2 52.9 %copy-start.15 = (s32[128]{0:T(128)S(1)}, s32[128]{0:T(128)}, u32[]{:S(2)}) copy-start(s32[128]{0:T(128)} %param.11) | copy-start | bytes 1540
  7.2 161.4 %all-gather.2.cloned.1.call-start = ((), (), s32[]{:S(2)}) async-start(), calls=%async_computation | async-start | bytes 34078720 | tf_op jit(solution)/shard_map/all_gather | solution.py:392
  10.0 9.3 %collective-permute-start.14 = (f32[2,16,512]{2,1,0:T(8,128)S(1)}, f32[2,16,512]{2,1,0:T(8,128)S(1)}, u32[]{:S(2)}, u32[]{:S(2)}) collective-permute-start(f32[2,16,512]{2,1,0:T(8,128)S(1)} %get-tuple-element.30), channel_id=1, source_target_pairs={{0,56},{4,12},{8,0},{12,20},{16,8},{20,28},{24,16},{28,36},{32,24}... | collective-permute-start | bytes 196616 | tf_op jit(solution)/shard_map/ppermute | solution.py:379
  12.6 6.8 %collective-permute-start.10 = (f32[2,16,512]{2,1,0:T(8,128)S(1)}, f32[2,16,512]{2,1,0:T(8,128)S(1)}, u32[]{:S(2)}, u32[]{:S(2)}) collective-permute-start(f32[2,16,512]{2,1,0:T(8,128)S(1)} %get-tuple-element.30), channel_id=1, source_target_pairs={{0,8},{4,60},{8,16},{12,4},{16,24},{20,12},{24,32},{28,20},{32,40}... | collective-permute-start | bytes 196616 | tf_op jit(solution)/shard_map/ppermute | solution.py:377
  16.6 5.4 %collective-permute-start = (f32[2,16,512]{2,1,0:T(8,128)S(1)}, f32[2,16,512]{2,1,0:T(8,128)S(1)}, u32[]{:S(2)}, u32[]{:S(2)}) collective-permute-start(f32[2,16,512]{2,1,0:T(8,128)S(1)} %get-tuple-element.33), channel_id=1, source_target_pairs={{0,64},{4,196},{8,72},{12,204},{16,80},{20,212},{24,88},{28,220},{... | collective-permute-start | bytes 196616 | tf_op jit(solution)/shard_map/ppermute | solution.py:377
  19.3 5.4 %collective-permute-start.2 = (f32[2,16,512]{2,1,0:T(8,128)S(1)}, f32[2,16,512]{2,1,0:T(8,128)S(1)}, u32[]{:S(2)}, u32[]{:S(2)}) collective-permute-start(f32[2,16,512]{2,1,0:T(8,128)S(1)} %get-tuple-element.33), channel_id=1, source_target_pairs={{0,192},{4,68},{8,200},{12,76},{16,208},{20,84},{24,216},{28,92},{... | collective-permute-start | bytes 196616 | tf_op jit(solution)/shard_map/ppermute | solution.py:379
  19.3 7.1 %collective-permute-start.15 = (f32[2,16,512]{2,1,0:T(8,128)S(1)}, f32[2,16,512]{2,1,0:T(8,128)S(1)}, u32[]{:S(2)}, u32[]{:S(2)}) collective-permute-start(f32[2,16,512]{2,1,0:T(8,128)S(1)} %collective-permute-done.14), channel_id=1, source_target_pairs={{0,56},{4,12},{8,0},{12,20},{16,8},{20,28},{24,16},{28,36},{32,24}... | collective-permute-start | bytes 196616 | tf_op jit(solution)/shard_map/ppermute | solution.py:379
  19.4 8.3 %collective-permute-start.11 = (f32[2,16,512]{2,1,0:T(8,128)S(1)}, f32[2,16,512]{2,1,0:T(8,128)S(1)}, u32[]{:S(2)}, u32[]{:S(2)}) collective-permute-start(f32[2,16,512]{2,1,0:T(8,128)S(1)} %collective-permute-done.10), channel_id=1, source_target_pairs={{0,8},{4,60},{8,16},{12,4},{16,24},{20,12},{24,32},{28,20},{32,40}... | collective-permute-start | bytes 196616 | tf_op jit(solution)/shard_map/ppermute | solution.py:377
  22.0 4.0 %collective-permute-start.1 = (f32[2,16,512]{2,1,0:T(8,128)S(1)}, f32[2,16,512]{2,1,0:T(8,128)S(1)}, u32[]{:S(2)}, u32[]{:S(2)}) collective-permute-start(f32[2,16,512]{2,1,0:T(8,128)S(1)} %collective-permute-done), channel_id=1, source_target_pairs={{0,64},{4,196},{8,72},{12,204},{16,80},{20,212},{24,88},{28,220},{... | collective-permute-start | bytes 196616 | tf_op jit(solution)/shard_map/ppermute | solution.py:377
  26.0 49.9 %copy-start.3 = (f32[8,16,512]{2,1,0:T(8,128)}, f32[8,16,512]{2,1,0:T(8,128)S(1)}, u32[]{:S(2)}) copy-start(f32[8,16,512]{2,1,0:T(8,128)S(1)} %pad_maximum_fusion.refs_0_) | copy-start | bytes 786436
  26.1 19.0 %collective-permute-start.3 = (f32[8,16,512]{2,1,0:T(8,128)S(1)}, f32[8,16,512]{2,1,0:T(8,128)S(1)}, u32[]{:S(2)}, u32[]{:S(2)}) collective-permute-start(f32[8,16,512]{2,1,0:T(8,128)S(1)} %pad_maximum_fusion.refs_0_), channel_id=1, source_target_pairs={{0,8},{4,60},{8,16},{12,4},{16,24},{20,12},{24,32},{28,20},{32,40}... | collective-permute-start | bytes 786440 | tf_op jit(solution)/shard_map/ppermute | solution.py:377
  26.5 14.3 %collective-permute-start.16 = (f32[2,16,512]{2,1,0:T(8,128)S(1)}, f32[2,16,512]{2,1,0:T(8,128)S(1)}, u32[]{:S(2)}, u32[]{:S(2)}) collective-permute-start(f32[2,16,512]{2,1,0:T(8,128)S(1)} %collective-permute-done.15), channel_id=1, source_target_pairs={{0,56},{4,12},{8,0},{12,20},{16,8},{20,28},{24,16},{28,36},{32,24}... | collective-permute-start | bytes 196616 | tf_op jit(solution)/shard_map/ppermute | solution.py:379
  27.6 8.8 %collective-permute-start.12 = (f32[2,16,512]{2,1,0:T(8,128)S(1)}, f32[2,16,512]{2,1,0:T(8,128)S(1)}, u32[]{:S(2)}, u32[]{:S(2)}) collective-permute-start(f32[2,16,512]{2,1,0:T(8,128)S(1)} %collective-permute-done.11), channel_id=1, source_target_pairs={{0,8},{4,60},{8,16},{12,4},{16,24},{20,12},{24,32},{28,20},{32,40}... | collective-permute-start | bytes 196616 | tf_op jit(solution)/shard_map/ppermute | solution.py:377
  36.4 4.4 %collective-permute-start.13 = (f32[2,16,512]{2,1,0:T(8,128)S(1)}, f32[2,16,512]{2,1,0:T(8,128)S(1)}, u32[]{:S(2)}, u32[]{:S(2)}) collective-permute-start(f32[2,16,512]{2,1,0:T(8,128)S(1)} %collective-permute-done.12), channel_id=1, source_target_pairs={{0,8},{4,60},{8,16},{12,4},{16,24},{20,12},{24,32},{28,20},{32,40}... | collective-permute-start | bytes 196616 | tf_op jit(solution)/shard_map/ppermute | solution.py:377
  40.8 35.1 %copy-start.4 = (f32[16,16,512]{2,1,0:T(8,128)}, f32[16,16,512]{2,1,0:T(8,128)S(1)}, u32[]{:S(2)}) copy-start(f32[16,16,512]{2,1,0:T(8,128)S(1)} %constant_dynamic-update-slice_fusion.refs_8_) | copy-start | bytes 1572868
  40.8 19.7 %collective-permute-start.17 = (f32[16,16,512]{2,1,0:T(8,128)S(1)}, f32[16,16,512]{2,1,0:T(8,128)S(1)}, u32[]{:S(2)}, u32[]{:S(2)}) collective-permute-start(f32[16,16,512]{2,1,0:T(8,128)S(1)} %constant_dynamic-update-slice_fusion.refs_8_), channel_id=1, source_target_pairs={{0,64},{4,196},{8,72},{12,204},{16,80},{20,212},{24,88},{28,220},{... | collective-permute-start | bytes 1572872 | tf_op jit(solution)/shard_map/ppermute | solution.py:377
  45.1 12.3 %collective-permute-start.7 = (f32[8,16,512]{2,1,0:T(8,128)S(1)}, f32[8,16,512]{2,1,0:T(8,128)S(1)}, u32[]{:S(2)}, u32[]{:S(2)}) collective-permute-start(f32[8,16,512]{2,1,0:T(8,128)S(1)} %pad_maximum_fusion.refs_0_), channel_id=1, source_target_pairs={{0,56},{4,12},{8,0},{12,20},{16,8},{20,28},{24,16},{28,36},{32,24}... | collective-permute-start | bytes 786440 | tf_op jit(solution)/shard_map/ppermute | solution.py:379
  45.1 30.9 %copy-start.8 = (f32[8,16,512]{2,1,0:T(8,128)}, f32[8,16,512]{2,1,0:T(8,128)S(1)}, u32[]{:S(2)}) copy-start(f32[8,16,512]{2,1,0:T(8,128)S(1)} %collective-permute-done.3.refs_1_) | copy-start | bytes 786436
  45.1 12.3 %collective-permute-start.4 = (f32[8,16,512]{2,1,0:T(8,128)S(1)}, f32[8,16,512]{2,1,0:T(8,128)S(1)}, u32[]{:S(2)}, u32[]{:S(2)}) collective-permute-start(f32[8,16,512]{2,1,0:T(8,128)S(1)} %collective-permute-done.3.refs_1_), channel_id=1, source_target_pairs={{0,8},{4,60},{8,16},{12,4},{16,24},{20,12},{24,32},{28,20},{32,40}... | collective-permute-start | bytes 786440 | tf_op jit(solution)/shard_map/ppermute | solution.py:377
  57.4 18.5 %copy-start.9 = (f32[8,16,512]{2,1,0:T(8,128)}, f32[8,16,512]{2,1,0:T(8,128)S(1)}, u32[]{:S(2)}) copy-start(f32[8,16,512]{2,1,0:T(8,128)S(1)} %collective-permute-done.7.refs_7_) | copy-start | bytes 786436
  57.4 7.6 %collective-permute-start.8 = (f32[8,16,512]{2,1,0:T(8,128)S(1)}, f32[8,16,512]{2,1,0:T(8,128)S(1)}, u32[]{:S(2)}, u32[]{:S(2)}) collective-permute-start(f32[8,16,512]{2,1,0:T(8,128)S(1)} %collective-permute-done.7.refs_7_), channel_id=1, source_target_pairs={{0,56},{4,12},{8,0},{12,20},{16,8},{20,28},{24,16},{28,36},{32,24}... | collective-permute-start | bytes 786440 | tf_op jit(solution)/shard_map/ppermute | solution.py:379
  57.5 18.5 %copy-start.10 = (f32[8,16,512]{2,1,0:T(8,128)}, f32[8,16,512]{2,1,0:T(8,128)S(1)}, u32[]{:S(2)}) copy-start(f32[8,16,512]{2,1,0:T(8,128)S(1)} %collective-permute-done.4.refs_2_) | copy-start | bytes 786436
  57.5 8.1 %collective-permute-start.5 = (f32[8,16,512]{2,1,0:T(8,128)S(1)}, f32[8,16,512]{2,1,0:T(8,128)}, u32[]{:S(2)}, u32[]{:S(2)}) collective-permute-start(f32[8,16,512]{2,1,0:T(8,128)S(1)} %collective-permute-done.4.refs_2_), channel_id=1, source_target_pairs={{0,8},{4,60},{8,16},{12,4},{16,24},{20,12},{24,32},{28,20},{32,40}... | collective-permute-start | bytes 786440 | tf_op jit(solution)/shard_map/ppermute | solution.py:377
  60.4 9.7 %collective-permute-start.19 = (f32[16,16,512]{2,1,0:T(8,128)S(1)}, f32[16,16,512]{2,1,0:T(8,128)S(1)}, u32[]{:S(2)}, u32[]{:S(2)}) collective-permute-start(f32[16,16,512]{2,1,0:T(8,128)S(1)} %constant_dynamic-update-slice_fusion.refs_8_), channel_id=1, source_target_pairs={{0,192},{4,68},{8,200},{12,76},{16,208},{20,84},{24,216},{28,92},{... | collective-permute-start | bytes 1572872 | tf_op jit(solution)/shard_map/ppermute | solution.py:379
  60.5 15.5 %copy-start.5 = (f32[16,16,512]{2,1,0:T(8,128)}, f32[16,16,512]{2,1,0:T(8,128)S(1)}, u32[]{:S(2)}) copy-start(f32[16,16,512]{2,1,0:T(8,128)S(1)} %collective-permute-done.17.refs_9_) | copy-start | bytes 1572868
  60.5 15.4 %collective-permute-start.18 = (f32[16,16,512]{2,1,0:T(8,128)S(1)}, f32[16,16,512]{2,1,0:T(8,128)S(1)}, u32[]{:S(2)}, u32[]{:S(2)}) collective-permute-start(f32[16,16,512]{2,1,0:T(8,128)S(1)} %collective-permute-done.17.refs_9_), channel_id=1, source_target_pairs={{0,64},{4,196},{8,72},{12,204},{16,80},{20,212},{24,88},{28,220},{... | collective-permute-start | bytes 1572872 | tf_op jit(solution)/shard_map/ppermute | solution.py:377
  65.0 11.0 %copy-start.11 = (f32[8,16,512]{2,1,0:T(8,128)}, f32[8,16,512]{2,1,0:T(8,128)S(1)}, u32[]{:S(2)}) copy-start(f32[8,16,512]{2,1,0:T(8,128)S(1)} %collective-permute-done.8.refs_6_) | copy-start | bytes 786436
  65.0 9.5 %collective-permute-start.9 = (f32[8,16,512]{2,1,0:T(8,128)S(1)}, f32[8,16,512]{2,1,0:T(8,128)S(1)}, u32[]{:S(2)}, u32[]{:S(2)}) collective-permute-start(f32[8,16,512]{2,1,0:T(8,128)S(1)} %collective-permute-done.8.refs_6_), channel_id=1, source_target_pairs={{0,56},{4,12},{8,0},{12,20},{16,8},{20,28},{24,16},{28,36},{32,24}... | collective-permute-start | bytes 786440 | tf_op jit(solution)/shard_map/ppermute | solution.py:379
  65.5 9.7 %collective-permute-start.6 = (f32[8,16,512]{2,1,0:T(8,128)}, f32[8,16,512]{2,1,0:T(8,128)S(1)}, u32[]{:S(2)}, u32[]{:S(2)}) collective-permute-start(f32[8,16,512]{2,1,0:T(8,128)} %collective-permute-done.5.refs_3_), channel_id=1, source_target_pairs={{0,8},{4,60},{8,16},{12,4},{16,24},{20,12},{24,32},{28,20},{32,40}... | collective-permute-start | bytes 786440 | tf_op jit(solution)/shard_map/ppermute | solution.py:377
  70.1 5.9 %copy-start.6 = (f32[16,16,512]{2,1,0:T(8,128)}, f32[16,16,512]{2,1,0:T(8,128)S(1)}, u32[]{:S(2)}) copy-start(f32[16,16,512]{2,1,0:T(8,128)S(1)} %collective-permute-done.19.refs_11_) | copy-start | bytes 1572868
  74.5 0.7 copy-start.12
  75.2 0.7 copy-start.13
  76.0 0.8 copy-start.7
  82.2 17.4 %collective-permute-start.20 = (f32[24,32,512]{2,1,0:T(8,128)}, f32[24,32,512]{2,1,0:T(8,128)S(1)}, u32[]{:S(2)}, u32[]{:S(2)}) collective-permute-start(f32[24,32,512]{2,1,0:T(8,128)} %get-tuple-element.25), channel_id=1, source_target_pairs={{0,4},{4,0},{8,12},{12,8},{16,20},{20,16},{24,28},{28,24},{32,36},... | collective-permute-start | bytes 4718600 | tf_op jit(solution)/shard_map/ppermute | solution.py:414
  101.3 31.2 %copy-start.1 = (f32[24,32,512]{2,1,0:T(8,128)}, f32[24,32,512]{2,1,0:T(8,128)S(1)}, u32[]{:S(2)}) copy-start(f32[24,32,512]{2,1,0:T(8,128)S(1)} %broadcast_select_fusion.p0) | copy-start | bytes 4718596
  101.3 31.2 %collective-permute-start.21 = (f32[24,32,512]{2,1,0:T(8,128)S(1)}, f32[24,32,512]{2,1,0:T(8,128)S(1)}, u32[]{:S(2)}, u32[]{:S(2)}) collective-permute-start(f32[24,32,512]{2,1,0:T(8,128)S(1)} %broadcast_select_fusion.p0), channel_id=1, source_target_pairs={{0,1},{1,2},{2,3},{3,0},{4,7},{5,4},{6,5},{7,6},{8,9},{9,10},{10,1... | collective-permute-start | bytes 4718600 | tf_op jit(solution)/shard_map/ppermute | solution.py:417
  132.5 36.1 %collective-permute-start.22 = (f32[24,32,512]{2,1,0:T(8,128)S(1)}, f32[24,32,512]{2,1,0:T(8,128)}, u32[]{:S(2)}, u32[]{:S(2)}) collective-permute-start(f32[24,32,512]{2,1,0:T(8,128)S(1)} %broadcast_select_fusion.p0), channel_id=1, source_target_pairs={{0,3},{1,0},{2,1},{3,2},{4,5},{5,6},{6,7},{7,4},{8,11},{9,8},{10,9... | collective-permute-start | bytes 4718600 | tf_op jit(solution)/shard_map/ppermute | solution.py:418
  132.5 13.4 %copy-start.2 = (f32[24,32,512]{2,1,0:T(8,128)}, f32[24,32,512]{2,1,0:T(8,128)S(1)}, u32[]{:S(2)}) copy-start(f32[24,32,512]{2,1,0:T(8,128)S(1)} %collective-permute-done.21.p1) | copy-start | bytes 4718596
  132.5 36.1 %collective-permute-start.23 = (f32[24,32,512]{2,1,0:T(8,128)S(1)}, f32[24,32,512]{2,1,0:T(8,128)}, u32[]{:S(2)}, u32[]{:S(2)}) collective-permute-start(f32[24,32,512]{2,1,0:T(8,128)S(1)} %collective-permute-done.21.p1), channel_id=1, source_target_pairs={{0,1},{1,2},{2,3},{3,0},{4,7},{5,4},{6,5},{7,6},{8,9},{9,10},{10,1... | collective-permute-start | bytes 4718600 | tf_op jit(solution)/shard_map/ppermute | solution.py:419
  135.2 13.3 %copy-start.14 = (s32[20,2]{0,1:T(2,128)S(1)}, s32[20,2]{0,1:T(2,128)}, u32[]{:S(2)}) copy-start(s32[20,2]{0,1:T(2,128)} %param.13) | copy-start | bytes 484
Sparse Core Ops, SparseCore 0:
  10.8 152.4 all-gather.1
where the time goes:
time: 199 us; the launch traced here: 197 us
  Pallas kernels  69.8 us (35%)
  starting transfers between devices  52.3 us (26%)
  waiting for transfers between devices  48.9 us (25%)
  between operations  14.4 us (7%)
  local copies, waits for them, and re-layouts  7.14 us (4%)
  other arithmetic  4.55 us (2%)
    ppermute x12, starting transfers between devices, ring(): near.append(lax.ppermute(near[-1], 'tiles', ahead))  28.9 us
    pallas_call x1, Pallas kernels, update_tiles(): pl.pallas_call(update_kernel, out_shape=jax.ShapeDtypeStruct(tiles.shape,...  21.7 us
    pallas_call x2, Pallas kernels, factorize(): pl.pallas_call(functools.partial(middle_kernel, at), out_shape=(full, dsh...  18.1 us
    ppermute x8, waiting for transfers between devices, ring(): far.append(lax.ppermute(far[-1], 'tiles', back))  17.5 us
    ppermute x1, waiting for transfers between devices, per_device(): other = lax.ppermute(mine, both, back)  14.9 us
    ppermute x1, starting transfers between devices, per_device(): lax.ppermute(theirs, 'tiles', swap)  13.4 us
    ppermute x12, waiting for transfers between devices, ring(): near.append(lax.ppermute(near[-1], 'tiles', ahead))  12.5 us
    pallas_call x1, Pallas kernels, factorize(): pl.pallas_call(functools.partial(last_kernel, 6), out_shape=(half, half,...  10.7 us
  transfers between devices with their start and end apart: 25, of which 9 were waited for; matrix products, arithmetic and copies ran while one was open for 4% of the time, Pallas kernels for 24%

commit v1 on v0

--- a/solution.py
+++ b/solution.py
@@ -268,9 +268,10 @@
         def rest(g):
             return pltpu.make_async_copy(table.at[info[4, g]], stage.at[g, pl.ds(b - tail, tail), :], sems.at[g])
 
-        @pl.loop(0, count)
+        @pl.loop(0, half)
         def _(g):
             rest(g).start()
+            rest(g + half).start()
 
         for c in parts:
             c.wait()
@@ -278,33 +279,21 @@
         @pl.loop(0, half)
         def _(g):
             rest(g).wait()
-            x = jnp.where(info[5, g] > 0, stage[g], 0.0)
-            xh, xl = split(x)
+            rest(g + half).wait()
+            xh, xl = split(jnp.where(info[5, g] > 0, stage[g], 0.0))
             yh, yl = split(dot3(xh, xl, full_high[...], full_low[...]))
             lh[g] = yh
             ll[g] = yl
-
-        @pl.loop(half, count)
-        def _(g):
-            rest(g).wait()
-            x = jnp.where(info[5, g] > 0, stage[g], 0.0)
-            xh, xl = split(x)
-            rh[g - half] = xh
-            rl[g - half] = xl
-
-    @pl.loop(0, tile.shape[0])
+            xh, xl = split(jnp.where(info[5, g + half] > 0, stage[g + half], 0.0))
+            rh[g] = xh
+            rl[g] = xl
+
+    @pl.loop(0, tile.shape[0], unroll=2)
     def _(t):
         slot = k * tile.shape[0] + t
-        live = info[2, slot] > 0
-
-        @pl.when(live)
-        def _():
-            i, j = info[0, slot], info[1, slot]
-            out[t] = tile[t] - dot3(lh[i], ll[i], rh[j], rl[j], nt=True)
-
-        @pl.when(jnp.logical_not(live))
-        def _():
-            out[t] = tile[t]
+        i, j = info[0, slot], info[1, slot]
+        product = dot3(lh[i], ll[i], rh[j], rl[j], nt=True)
+        out[t] = tile[t] - jnp.where(info[2, slot] > 0, product, 0.0)
 
 
 def update_tiles(tiles, full_high, full_low, parts, quarters, table, slots, valid, pairs):

time: 199 us -> 198 us (level)
  no operation moved by 1% of the time
where the time goes in v1:
time: 198 us; the launch traced here: 197 us
  Pallas kernels  69.9 us (35%)
  starting transfers between devices  52.3 us (26%)
  waiting for transfers between devices  48.9 us (25%)
  between operations  14.4 us (7%)
  local copies, waits for them, and re-layouts  7.14 us (4%)
  other arithmetic  4.55 us (2%)
    ppermute x12, starting transfers between devices, ring(): near.append(lax.ppermute(near[-1], 'tiles', ahead))  28.9 us
    pallas_call x1, Pallas kernels, update_tiles(): pl.pallas_call(update_kernel, out_shape=jax.ShapeDtypeStruct(tiles.shape,...  21.7 us
    pallas_call x2, Pallas kernels, factorize(): pl.pallas_call(functools.partial(middle_kernel, at), out_shape=(full, dsh...  18.1 us
    ppermute x8, waiting for transfers between devices, ring(): far.append(lax.ppermute(far[-1], 'tiles', back))  17.5 us
    ppermute x1, waiting for transfers between devices, per_device(): other = lax.ppermute(mine, both, back)  14.9 us
    ppermute x1, starting transfers between devices, per_device(): lax.ppermute(theirs, 'tiles', swap)  13.4 us
    ppermute x12, waiting for transfers between devices, ring(): near.append(lax.ppermute(near[-1], 'tiles', ahead))  12.5 us
    pallas_call x1, Pallas kernels, factorize(): pl.pallas_call(functools.partial(last_kernel, 6), out_shape=(half, half,...  10.7 us
  transfers between devices with their start and end apart: 25, of which 9 were waited for; matrix products, arithmetic and copies ran while one was open for 4% of the time, Pallas kernels for 24%

profile of v1, /device:TPU:1, one launch (start us, length us, event | category | flops | bytes accessed | tf_op | source)
XLA Modules:
  0.0 197.1 jit_solution(8635379430630505844)
XLA Ops:
  7.2 0.0 copy-start
  7.2 0.0 all-gather.2.cloned.1.call-start
  7.2 1.9 slice.16
  9.1 0.0 all-gather.2.cloned.1.call-update
  9.1 0.9 constant_dynamic-update-slice_fusion.7
  10.0 2.5 %collective-permute-start.14 = (f32[2,16,512]{2,1,0:T(8,128)S(1)}, f32[2,16,512]{2,1,0:T(8,128)S(1)}, u32[]{:S(2)}, u32[]{:S(2)}) collective-permute-start(f32[2,16,512]{2,1,0:T(8,128)S(1)} %get-tuple-element.30), channel_id=1, source_target_pairs={{0,56},{4,12},{8,0},{12,20},{16,8},{20,28},{24,16},{28,36},{32,24}... | collective-permute-start | bytes 196616 | tf_op jit(solution)/shard_map/ppermute | solution.py:368
  12.6 4.0 %collective-permute-start.10 = (f32[2,16,512]{2,1,0:T(8,128)S(1)}, f32[2,16,512]{2,1,0:T(8,128)S(1)}, u32[]{:S(2)}, u32[]{:S(2)}) collective-permute-start(f32[2,16,512]{2,1,0:T(8,128)S(1)} %get-tuple-element.30), channel_id=1, source_target_pairs={{0,8},{4,60},{8,16},{12,4},{16,24},{20,12},{24,32},{28,20},{32,40}... | collective-permute-start | bytes 196616 | tf_op jit(solution)/shard_map/ppermute | solution.py:366
  16.6 2.7 %collective-permute-start = (f32[2,16,512]{2,1,0:T(8,128)S(1)}, f32[2,16,512]{2,1,0:T(8,128)S(1)}, u32[]{:S(2)}, u32[]{:S(2)}) collective-permute-start(f32[2,16,512]{2,1,0:T(8,128)S(1)} %get-tuple-element.33), channel_id=1, source_target_pairs={{0,64},{4,196},{8,72},{12,204},{16,80},{20,212},{24,88},{28,220},{... | collective-permute-start | bytes 196616 | tf_op jit(solution)/shard_map/ppermute | solution.py:366
  19.3 0.0 collective-permute-start.2
  19.3 0.0 collective-permute-done.14
  19.3 0.0 collective-permute-start.15
  19.4 2.7 %collective-permute-start.11 = (f32[2,16,512]{2,1,0:T(8,128)S(1)}, f32[2,16,512]{2,1,0:T(8,128)S(1)}, u32[]{:S(2)}, u32[]{:S(2)}) collective-permute-start(f32[2,16,512]{2,1,0:T(8,128)S(1)} %collective-permute-done.10), channel_id=1, source_target_pairs={{0,8},{4,60},{8,16},{12,4},{16,24},{20,12},{24,32},{28,20},{32,40}... | collective-permute-start | bytes 196616 | tf_op jit(solution)/shard_map/ppermute | solution.py:366
  22.0 2.7 %collective-permute-start.1 = (f32[2,16,512]{2,1,0:T(8,128)S(1)}, f32[2,16,512]{2,1,0:T(8,128)S(1)}, u32[]{:S(2)}, u32[]{:S(2)}) collective-permute-start(f32[2,16,512]{2,1,0:T(8,128)S(1)} %collective-permute-done), channel_id=1, source_target_pairs={{0,64},{4,196},{8,72},{12,204},{16,80},{20,212},{24,88},{28,220},{... | collective-permute-start | bytes 196616 | tf_op jit(solution)/shard_map/ppermute | solution.py:366
  24.7 1.3 collective-permute-done.1
  26.1 0.4 collective-permute-start.3
  26.5 0.0 collective-permute-done.15
  26.5 1.1 collective-permute-start.16
  27.6 1.5 collective-permute-start.12
  29.2 7.2 %collective-permute-done.12 = f32[2,16,512]{2,1,0:T(8,128)S(1)} collective-permute-done((f32[2,16,512]{2,1,0:T(8,128)S(1)}, f32[2,16,512]{2,1,0:T(8,128)S(1)}, u32[]{:S(2)}, u32[]{:S(2)}) %collective-permute-start.12) | collective-permute-done | bytes 65568 | tf_op jit(solution)/shard_map/ppermute | solution.py:366
  36.4 0.4 collective-permute-start.13
  36.8 3.9 %collective-permute-done.13 = f32[2,16,512]{2,1,0:T(8,128)S(1)} collective-permute-done((f32[2,16,512]{2,1,0:T(8,128)S(1)}, f32[2,16,512]{2,1,0:T(8,128)S(1)}, u32[]{:S(2)}, u32[]{:S(2)}) %collective-permute-start.13) | collective-permute-done | bytes 65568 | tf_op jit(solution)/shard_map/ppermute | solution.py:366
  40.8 0.0 collective-permute-done.16
  40.8 0.0 copy-start.4
  40.8 4.3 %collective-permute-start.17 = (f32[16,16,512]{2,1,0:T(8,128)S(1)}, f32[16,16,512]{2,1,0:T(8,128)S(1)}, u32[]{:S(2)}, u32[]{:S(2)}) collective-permute-start(f32[16,16,512]{2,1,0:T(8,128)S(1)} %constant_dynamic-update-slice_fusion.refs_8_), channel_id=1, source_target_pairs={{0,64},{4,196},{8,72},{12,204},{16,80},{20,212},{24,88},{28,220},{... | collective-permute-start | bytes 1572872 | tf_op jit(solution)/shard_map/ppermute | solution.py:366
  45.1 0.0 collective-permute-start.7
  45.1 2.7 %collective-permute-start.4 = (f32[8,16,512]{2,1,0:T(8,128)S(1)}, f32[8,16,512]{2,1,0:T(8,128)S(1)}, u32[]{:S(2)}, u32[]{:S(2)}) collective-permute-start(f32[8,16,512]{2,1,0:T(8,128)S(1)} %collective-permute-done.3.refs_1_), channel_id=1, source_target_pairs={{0,8},{4,60},{8,16},{12,4},{16,24},{20,12},{24,32},{28,20},{32,40}... | collective-permute-start | bytes 786440 | tf_op jit(solution)/shard_map/ppermute | solution.py:366
  47.8 0.1 constant_dynamic-slice_fusion.3
  47.8 0.1 copy.20
  47.9 9.5 %collective-permute-done.7.refs_7_ = f32[8,16,512]{2,1,0:T(8,128)S(1)} collective-permute-done((f32[8,16,512]{2,1,0:T(8,128)S(1)}, f32[8,16,512]{2,1,0:T(8,128)S(1)}, u32[]{:S(2)}, u32[]{:S(2)}) %collective-permute-start.7) | collective-permute-done | bytes 262176 | tf_op jit(solution)/shard_map/ppermute | solution.py:368
  57.4 0.0 collective-permute-start.8
  57.5 2.7 %collective-permute-start.5 = (f32[8,16,512]{2,1,0:T(8,128)S(1)}, f32[8,16,512]{2,1,0:T(8,128)}, u32[]{:S(2)}, u32[]{:S(2)}) collective-permute-start(f32[8,16,512]{2,1,0:T(8,128)S(1)} %collective-permute-done.4.refs_2_), channel_id=1, source_target_pairs={{0,8},{4,60},{8,16},{12,4},{16,24},{20,12},{24,32},{28,20},{32,40}... | collective-permute-start | bytes 786440 | tf_op jit(solution)/shard_map/ppermute | solution.py:366
  60.1 0.2 select_reduce_fusion
  60.4 0.1 collective-permute-start.19
  60.5 2.6 %collective-permute-start.18 = (f32[16,16,512]{2,1,0:T(8,128)S(1)}, f32[16,16,512]{2,1,0:T(8,128)S(1)}, u32[]{:S(2)}, u32[]{:S(2)}) collective-permute-start(f32[16,16,512]{2,1,0:T(8,128)S(1)} %collective-permute-done.17.refs_9_), channel_id=1, source_target_pairs={{0,64},{4,196},{8,72},{12,204},{16,80},{20,212},{24,88},{28,220},{... | collective-permute-start | bytes 1572872 | tf_op jit(solution)/shard_map/ppermute | solution.py:366
  63.2 1.8 collective-permute-done.8.refs_6_
  65.0 0.5 collective-permute-start.9
  65.5 2.1 %collective-permute-start.6 = (f32[8,16,512]{2,1,0:T(8,128)}, f32[8,16,512]{2,1,0:T(8,128)S(1)}, u32[]{:S(2)}, u32[]{:S(2)}) collective-permute-start(f32[8,16,512]{2,1,0:T(8,128)} %collective-permute-done.5.refs_3_), channel_id=1, source_target_pairs={{0,8},{4,60},{8,16},{12,4},{16,24},{20,12},{24,32},{28,20},{32,40}... | collective-permute-start | bytes 786440 | tf_op jit(solution)/shard_map/ppermute | solution.py:366
  67.7 0.6 pad_add_fusion.place
  68.3 1.8 collective-permute-done.19.refs_11_
  70.1 4.4 %collective-permute-done.9.refs_5_ = f32[8,16,512]{2,1,0:T(8,128)S(1)} collective-permute-done((f32[8,16,512]{2,1,0:T(8,128)S(1)}, f32[8,16,512]{2,1,0:T(8,128)S(1)}, u32[]{:S(2)}, u32[]{:S(2)}) %collective-permute-start.9) | collective-permute-done | bytes 262176 | tf_op jit(solution)/shard_map/ppermute | solution.py:368
  74.5 0.7 copy-done.12
  75.2 0.7 copy-done.13
  76.0 0.8 copy-done.7
  76.8 5.4 %pick.1 = (f32[24,32,512]{2,1,0:T(8,128)}, f32[24,32,512]{2,1,0:T(8,128)}) custom-call(s32[2,3,24]{2,1,0:T(4,128)} %pad_add_fusion.place, f32[8,16,512]{2,1,0:T(8,128)} %copy-done.3, f32[8,16,512]{2,1,0:T(8,128)} %copy-done.8, f32[8,16,512]{2,1,0:T(8,128)} %copy-done.10, f32[8,16,512]{2,1,0:T(8,128)} %collective-permute-done.5.refs_3_, ...), custom_call_target="tpu_custom_call" | custom-call | bytes 6291456 | tf_op jit(solution)/shard_map/pick/pallas_call | solution.py:237
  82.2 13.4 %collective-permute-start.20 = (f32[24,32,512]{2,1,0:T(8,128)}, f32[24,32,512]{2,1,0:T(8,128)S(1)}, u32[]{:S(2)}, u32[]{:S(2)}) collective-permute-start(f32[24,32,512]{2,1,0:T(8,128)} %get-tuple-element.25), channel_id=1, source_target_pairs={{0,4},{4,0},{8,12},{12,8},{16,20},{20,16},{24,28},{28,24},{32,36},... | collective-permute-start | bytes 4718600 | tf_op jit(solution)/shard_map/ppermute | solution.py:403
  95.7 4.0 %collective-permute-done.20 = f32[24,32,512]{2,1,0:T(8,128)S(1)} collective-permute-done((f32[24,32,512]{2,1,0:T(8,128)}, f32[24,32,512]{2,1,0:T(8,128)S(1)}, u32[]{:S(2)}, u32[]{:S(2)}) %collective-permute-start.20) | collective-permute-done | bytes 1572896 | tf_op jit(solution)/shard_map/ppermute | solution.py:403
  99.6 1.7 broadcast_select_fusion.p0
  101.3 3.0 %collective-permute-start.21 = (f32[24,32,512]{2,1,0:T(8,128)S(1)}, f32[24,32,512]{2,1,0:T(8,128)S(1)}, u32[]{:S(2)}, u32[]{:S(2)}) collective-permute-start(f32[24,32,512]{2,1,0:T(8,128)S(1)} %broadcast_select_fusion.p0), channel_id=1, source_target_pairs={{0,1},{1,2},{2,3},{3,0},{4,7},{5,4},{6,5},{7,6},{8,9},{9,10},{10,1... | collective-permute-start | bytes 4718600 | tf_op jit(solution)/shard_map/ppermute | solution.py:406
  104.3 10.1 %panels0.1 = (f32[512,512]{1,0:T(8,128)}, f32[1,128]{1,0:T(1,128)}) custom-call(f32[2,256,256]{2,1,0:T(8,128)} %pivot.1, f32[256,256]{1,0:T(8,128)} %coupling.1), custom_call_target="tpu_custom_call" | custom-call | flops 6000000000 | bytes 2097152 | tf_op jit(solution)/shard_map/panels0/pallas_call | solution.py:142
  114.4 9.4 %shard_map.94 = (f32[512,512]{1,0:T(8,128)}, f32[1,128]{1,0:T(1,128)}) custom-call(f32[512,512]{1,0:T(8,128)} %get-tuple-element.16.before), custom_call_target="tpu_custom_call" | custom-call | flops 6000000000 | bytes 2097152 | tf_op jit(solution)/shard_map/pallas_call | solution.py:147
  123.8 8.7 %shard_map.95 = (f32[512,512]{1,0:T(8,128)}, f32[1,128]{1,0:T(1,128)}) custom-call(f32[512,512]{1,0:T(8,128)} %get-tuple-element.17.before), custom_call_target="tpu_custom_call" | custom-call | flops 6000000000 | bytes 2097152 | tf_op jit(solution)/shard_map/pallas_call | solution.py:147
  132.5 2.7 %collective-permute-start.23 = (f32[24,32,512]{2,1,0:T(8,128)S(1)}, f32[24,32,512]{2,1,0:T(8,128)}, u32[]{:S(2)}, u32[]{:S(2)}) collective-permute-start(f32[24,32,512]{2,1,0:T(8,128)S(1)} %collective-permute-done.21.p1), channel_id=1, source_target_pairs={{0,1},{1,2},{2,3},{3,0},{4,7},{5,4},{6,5},{7,6},{8,9},{9,10},{10,1... | collective-permute-start | bytes 4718600 | tf_op jit(solution)/shard_map/ppermute | solution.py:408
  135.2 10.7 %panels6.1 = (bf16[512,512]{1,0:T(8,128)(2,1)}, bf16[512,512]{1,0:T(8,128)(2,1)}, bf16[512,512]{1,0:T(8,128)(2,1)}, bf16[512,512]{1,0:T(8,128)(2,1)}, f32[1,512]{1,0:T(1,128)}) custom-call(f32[512,512]{1,0:T(8,128)} %get-tuple-element.18.before, f32[1,128]{1,0:T(1,128)} %get-tuple-element.19.d0, f32[1,128]{1,0:T(1,128)} %get-tuple-element.20.d1, ...), custom_call_target="tpu_custom_call" | custom-call | flops 6000000000 | bytes 2097152 | tf_op jit(solution)/shard_map/panels6/pallas_call | solution.py:151
  145.9 0.1 constant_dynamic-slice_fusion.2
  146.0 0.1 copy.25
  146.1 0.5 broadcast.169
  146.6 1.3 reduce.3
  147.9 0.6 reshape.62
  148.6 0.1 pad_add_fusion.1
  148.6 0.6 stack.57.info
  149.3 0.6 compare_convert_fusion.keep
  149.9 3.8 %own_factors.1 = f32[2,256,512]{2,1,0:T(8,128)} custom-call(s32[2]{0:T(128)} %compare_convert_fusion.keep, f32[2,256,512]{2,1,0:T(8,128)} %x.9, bf16[512,512]{1,0:T(8,128)(2,1)} %get-tuple-element.26.high, bf16[512,512]{1,0:T(8,128)(2,1)} %get-tuple-element.27.low, f32[1,512]{1,0:T(1,128)} %get-tuple-element.28.diag), custom_call_target="tpu_custom_call" | custom-call | flops 805306368 | bytes 2097152 | tf_op jit(solution)/shard_map/own_factors/pallas_call | solution.py:177
  153.7 14.9 %collective-permute-done.22.p2 = f32[24,32,512]{2,1,0:T(8,128)} collective-permute-done((f32[24,32,512]{2,1,0:T(8,128)S(1)}, f32[24,32,512]{2,1,0:T(8,128)}, u32[]{:S(2)}, u32[]{:S(2)}) %collective-permute-start.22) | collective-permute-done | bytes 1572896 | tf_op jit(solution)/shard_map/ppermute | solution.py:407
  168.6 21.7 %update_tiles.1 = f32[20,256,256]{2,1,0:T(8,128)} custom-call(s32[6,24]{1,0:T(8,128)} %stack.57.info, f32[20,256,256]{2,1,0:T(8,128)} %tile.1, bf16[512,512]{1,0:T(8,128)(2,1)} %get-tuple-element.22.full_high, bf16[512,512]{1,0:T(8,128)(2,1)} %get-tuple-element.23.full_low, f32[24,32,512]{2,1,0:T(8,128)} %copy-done.1, f32[24,32,512]{2,1,0:T(8,128)} %copy-done.2, ...), custom_call_target="tpu_custom_call" | custom-call | flops 8858370048 | bytes 23068672 | tf_op jit(solution)/shard_map/update_tiles/pallas_call | solution.py:321
  (60 shorter events, 0.3 us)
Async XLA Ops:
  7.2 40.6 %copy-start = (s32[64,24]{0,1:T(8,128)S(1)}, s32[64,24]{0,1:T(8,128)}, u32[]{:S(2)}) copy-start(s32[64,24]{0,1:T(8,128)} %param.12) | copy-start | bytes 18436
  7.2 52.9 %copy-start.15 = (s32[128]{0:T(128)S(1)}, s32[128]{0:T(128)}, u32[]{:S(2)}) copy-start(s32[128]{0:T(128)} %param.11) | copy-start | bytes 1540
  7.2 161.4 %all-gather.2.cloned.1.call-start = ((), (), s32[]{:S(2)}) async-start(), calls=%async_computation | async-start | bytes 34078720 | tf_op jit(solution)/shard_map/all_gather | solution.py:381
  10.0 9.3 %collective-permute-start.14 = (f32[2,16,512]{2,1,0:T(8,128)S(1)}, f32[2,16,512]{2,1,0:T(8,128)S(1)}, u32[]{:S(2)}, u32[]{:S(2)}) collective-permute-start(f32[2,16,512]{2,1,0:T(8,128)S(1)} %get-tuple-element.30), channel_id=1, source_target_pairs={{0,56},{4,12},{8,0},{12,20},{16,8},{20,28},{24,16},{28,36},{32,24}... | collective-permute-start | bytes 196616 | tf_op jit(solution)/shard_map/ppermute | solution.py:368
  12.6 6.8 %collective-permute-start.10 = (f32[2,16,512]{2,1,0:T(8,128)S(1)}, f32[2,16,512]{2,1,0:T(8,128)S(1)}, u32[]{:S(2)}, u32[]{:S(2)}) collective-permute-start(f32[2,16,512]{2,1,0:T(8,128)S(1)} %get-tuple-element.30), channel_id=1, source_target_pairs={{0,8},{4,60},{8,16},{12,4},{16,24},{20,12},{24,32},{28,20},{32,40}... | collective-permute-start | bytes 196616 | tf_op jit(solution)/shard_map/ppermute | solution.py:366
  16.6 5.4 %collective-permute-start = (f32[2,16,512]{2,1,0:T(8,128)S(1)}, f32[2,16,512]{2,1,0:T(8,128)S(1)}, u32[]{:S(2)}, u32[]{:S(2)}) collective-permute-start(f32[2,16,512]{2,1,0:T(8,128)S(1)} %get-tuple-element.33), channel_id=1, source_target_pairs={{0,64},{4,196},{8,72},{12,204},{16,80},{20,212},{24,88},{28,220},{... | collective-permute-start | bytes 196616 | tf_op jit(solution)/shard_map/ppermute | solution.py:366
  19.3 5.4 %collective-permute-start.2 = (f32[2,16,512]{2,1,0:T(8,128)S(1)}, f32[2,16,512]{2,1,0:T(8,128)S(1)}, u32[]{:S(2)}, u32[]{:S(2)}) collective-permute-start(f32[2,16,512]{2,1,0:T(8,128)S(1)} %get-tuple-element.33), channel_id=1, source_target_pairs={{0,192},{4,68},{8,200},{12,76},{16,208},{20,84},{24,216},{28,92},{... | collective-permute-start | bytes 196616 | tf_op jit(solution)/shard_map/ppermute | solution.py:368
  19.3 7.1 %collective-permute-start.15 = (f32[2,16,512]{2,1,0:T(8,128)S(1)}, f32[2,16,512]{2,1,0:T(8,128)S(1)}, u32[]{:S(2)}, u32[]{:S(2)}) collective-permute-start(f32[2,16,512]{2,1,0:T(8,128)S(1)} %collective-permute-done.14), channel_id=1, source_target_pairs={{0,56},{4,12},{8,0},{12,20},{16,8},{20,28},{24,16},{28,36},{32,24}... | collective-permute-start | bytes 196616 | tf_op jit(solution)/shard_map/ppermute | solution.py:368
  19.4 8.3 %collective-permute-start.11 = (f32[2,16,512]{2,1,0:T(8,128)S(1)}, f32[2,16,512]{2,1,0:T(8,128)S(1)}, u32[]{:S(2)}, u32[]{:S(2)}) collective-permute-start(f32[2,16,512]{2,1,0:T(8,128)S(1)} %collective-permute-done.10), channel_id=1, source_target_pairs={{0,8},{4,60},{8,16},{12,4},{16,24},{20,12},{24,32},{28,20},{32,40}... | collective-permute-start | bytes 196616 | tf_op jit(solution)/shard_map/ppermute | solution.py:366
  22.0 4.0 %collective-permute-start.1 = (f32[2,16,512]{2,1,0:T(8,128)S(1)}, f32[2,16,512]{2,1,0:T(8,128)S(1)}, u32[]{:S(2)}, u32[]{:S(2)}) collective-permute-start(f32[2,16,512]{2,1,0:T(8,128)S(1)} %collective-permute-done), channel_id=1, source_target_pairs={{0,64},{4,196},{8,72},{12,204},{16,80},{20,212},{24,88},{28,220},{... | collective-permute-start | bytes 196616 | tf_op jit(solution)/shard_map/ppermute | solution.py:366
  26.0 49.9 %copy-start.3 = (f32[8,16,512]{2,1,0:T(8,128)}, f32[8,16,512]{2,1,0:T(8,128)S(1)}, u32[]{:S(2)}) copy-start(f32[8,16,512]{2,1,0:T(8,128)S(1)} %pad_maximum_fusion.refs_0_) | copy-start | bytes 786436
  26.1 19.0 %collective-permute-start.3 = (f32[8,16,512]{2,1,0:T(8,128)S(1)}, f32[8,16,512]{2,1,0:T(8,128)S(1)}, u32[]{:S(2)}, u32[]{:S(2)}) collective-permute-start(f32[8,16,512]{2,1,0:T(8,128)S(1)} %pad_maximum_fusion.refs_0_), channel_id=1, source_target_pairs={{0,8},{4,60},{8,16},{12,4},{16,24},{20,12},{24,32},{28,20},{32,40}... | collective-permute-start | bytes 786440 | tf_op jit(solution)/shard_map/ppermute | solution.py:366
  26.5 14.3 %collective-permute-start.16 = (f32[2,16,512]{2,1,0:T(8,128)S(1)}, f32[2,16,512]{2,1,0:T(8,128)S(1)}, u32[]{:S(2)}, u32[]{:S(2)}) collective-permute-start(f32[2,16,512]{2,1,0:T(8,128)S(1)} %collective-permute-done.15), channel_id=1, source_target_pairs={{0,56},{4,12},{8,0},{12,20},{16,8},{20,28},{24,16},{28,36},{32,24}... | collective-permute-start | bytes 196616 | tf_op jit(solution)/shard_map/ppermute | solution.py:368
  27.6 8.8 %collective-permute-start.12 = (f32[2,16,512]{2,1,0:T(8,128)S(1)}, f32[2,16,512]{2,1,0:T(8,128)S(1)}, u32[]{:S(2)}, u32[]{:S(2)}) collective-permute-start(f32[2,16,512]{2,1,0:T(8,128)S(1)} %collective-permute-done.11), channel_id=1, source_target_pairs={{0,8},{4,60},{8,16},{12,4},{16,24},{20,12},{24,32},{28,20},{32,40}... | collective-permute-start | bytes 196616 | tf_op jit(solution)/shard_map/ppermute | solution.py:366
  36.4 4.4 %collective-permute-start.13 = (f32[2,16,512]{2,1,0:T(8,128)S(1)}, f32[2,16,512]{2,1,0:T(8,128)S(1)}, u32[]{:S(2)}, u32[]{:S(2)}) collective-permute-start(f32[2,16,512]{2,1,0:T(8,128)S(1)} %collective-permute-done.12), channel_id=1, source_target_pairs={{0,8},{4,60},{8,16},{12,4},{16,24},{20,12},{24,32},{28,20},{32,40}... | collective-permute-start | bytes 196616 | tf_op jit(solution)/shard_map/ppermute | solution.py:366
  40.8 35.1 %copy-start.4 = (f32[16,16,512]{2,1,0:T(8,128)}, f32[16,16,512]{2,1,0:T(8,128)S(1)}, u32[]{:S(2)}) copy-start(f32[16,16,512]{2,1,0:T(8,128)S(1)} %constant_dynamic-update-slice_fusion.refs_8_) | copy-start | bytes 1572868
  40.8 19.7 %collective-permute-start.17 = (f32[16,16,512]{2,1,0:T(8,128)S(1)}, f32[16,16,512]{2,1,0:T(8,128)S(1)}, u32[]{:S(2)}, u32[]{:S(2)}) collective-permute-start(f32[16,16,512]{2,1,0:T(8,128)S(1)} %constant_dynamic-update-slice_fusion.refs_8_), channel_id=1, source_target_pairs={{0,64},{4,196},{8,72},{12,204},{16,80},{20,212},{24,88},{28,220},{... | collective-permute-start | bytes 1572872 | tf_op jit(solution)/shard_map/ppermute | solution.py:366
  45.1 12.3 %collective-permute-start.7 = (f32[8,16,512]{2,1,0:T(8,128)S(1)}, f32[8,16,512]{2,1,0:T(8,128)S(1)}, u32[]{:S(2)}, u32[]{:S(2)}) collective-permute-start(f32[8,16,512]{2,1,0:T(8,128)S(1)} %pad_maximum_fusion.refs_0_), channel_id=1, source_target_pairs={{0,56},{4,12},{8,0},{12,20},{16,8},{20,28},{24,16},{28,36},{32,24}... | collective-permute-start | bytes 786440 | tf_op jit(solution)/shard_map/ppermute | solution.py:368
  45.1 30.9 %copy-start.8 = (f32[8,16,512]{2,1,0:T(8,128)}, f32[8,16,512]{2,1,0:T(8,128)S(1)}, u32[]{:S(2)}) copy-start(f32[8,16,512]{2,1,0:T(8,128)S(1)} %collective-permute-done.3.refs_1_) | copy-start | bytes 786436
  45.1 12.3 %collective-permute-start.4 = (f32[8,16,512]{2,1,0:T(8,128)S(1)}, f32[8,16,512]{2,1,0:T(8,128)S(1)}, u32[]{:S(2)}, u32[]{:S(2)}) collective-permute-start(f32[8,16,512]{2,1,0:T(8,128)S(1)} %collective-permute-done.3.refs_1_), channel_id=1, source_target_pairs={{0,8},{4,60},{8,16},{12,4},{16,24},{20,12},{24,32},{28,20},{32,40}... | collective-permute-start | bytes 786440 | tf_op jit(solution)/shard_map/ppermute | solution.py:366
  57.4 18.5 %copy-start.9 = (f32[8,16,512]{2,1,0:T(8,128)}, f32[8,16,512]{2,1,0:T(8,128)S(1)}, u32[]{:S(2)}) copy-start(f32[8,16,512]{2,1,0:T(8,128)S(1)} %collective-permute-done.7.refs_7_) | copy-start | bytes 786436
  57.4 7.6 %collective-permute-start.8 = (f32[8,16,512]{2,1,0:T(8,128)S(1)}, f32[8,16,512]{2,1,0:T(8,128)S(1)}, u32[]{:S(2)}, u32[]{:S(2)}) collective-permute-start(f32[8,16,512]{2,1,0:T(8,128)S(1)} %collective-permute-done.7.refs_7_), channel_id=1, source_target_pairs={{0,56},{4,12},{8,0},{12,20},{16,8},{20,28},{24,16},{28,36},{32,24}... | collective-permute-start | bytes 786440 | tf_op jit(solution)/shard_map/ppermute | solution.py:368
  57.5 18.5 %copy-start.10 = (f32[8,16,512]{2,1,0:T(8,128)}, f32[8,16,512]{2,1,0:T(8,128)S(1)}, u32[]{:S(2)}) copy-start(f32[8,16,512]{2,1,0:T(8,128)S(1)} %collective-permute-done.4.refs_2_) | copy-start | bytes 786436
  57.5 8.1 %collective-permute-start.5 = (f32[8,16,512]{2,1,0:T(8,128)S(1)}, f32[8,16,512]{2,1,0:T(8,128)}, u32[]{:S(2)}, u32[]{:S(2)}) collective-permute-start(f32[8,16,512]{2,1,0:T(8,128)S(1)} %collective-permute-done.4.refs_2_), channel_id=1, source_target_pairs={{0,8},{4,60},{8,16},{12,4},{16,24},{20,12},{24,32},{28,20},{32,40}... | collective-permute-start | bytes 786440 | tf_op jit(solution)/shard_map/ppermute | solution.py:366
  60.4 9.7 %collective-permute-start.19 = (f32[16,16,512]{2,1,0:T(8,128)S(1)}, f32[16,16,512]{2,1,0:T(8,128)S(1)}, u32[]{:S(2)}, u32[]{:S(2)}) collective-permute-start(f32[16,16,512]{2,1,0:T(8,128)S(1)} %constant_dynamic-update-slice_fusion.refs_8_), channel_id=1, source_target_pairs={{0,192},{4,68},{8,200},{12,76},{16,208},{20,84},{24,216},{28,92},{... | collective-permute-start | bytes 1572872 | tf_op jit(solution)/shard_map/ppermute | solution.py:368
  60.5 15.5 %copy-start.5 = (f32[16,16,512]{2,1,0:T(8,128)}, f32[16,16,512]{2,1,0:T(8,128)S(1)}, u32[]{:S(2)}) copy-start(f32[16,16,512]{2,1,0:T(8,128)S(1)} %collective-permute-done.17.refs_9_) | copy-start | bytes 1572868
  60.5 15.4 %collective-permute-start.18 = (f32[16,16,512]{2,1,0:T(8,128)S(1)}, f32[16,16,512]{2,1,0:T(8,128)S(1)}, u32[]{:S(2)}, u32[]{:S(2)}) collective-permute-start(f32[16,16,512]{2,1,0:T(8,128)S(1)} %collective-permute-done.17.refs_9_), channel_id=1, source_target_pairs={{0,64},{4,196},{8,72},{12,204},{16,80},{20,212},{24,88},{28,220},{... | collective-permute-start | bytes 1572872 | tf_op jit(solution)/shard_map/ppermute | solution.py:366
  65.0 11.0 %copy-start.11 = (f32[8,16,512]{2,1,0:T(8,128)}, f32[8,16,512]{2,1,0:T(8,128)S(1)}, u32[]{:S(2)}) copy-start(f32[8,16,512]{2,1,0:T(8,128)S(1)} %collective-permute-done.8.refs_6_) | copy-start | bytes 786436
  65.0 9.5 %collective-permute-start.9 = (f32[8,16,512]{2,1,0:T(8,128)S(1)}, f32[8,16,512]{2,1,0:T(8,128)S(1)}, u32[]{:S(2)}, u32[]{:S(2)}) collective-permute-start(f32[8,16,512]{2,1,0:T(8,128)S(1)} %collective-permute-done.8.refs_6_), channel_id=1, source_target_pairs={{0,56},{4,12},{8,0},{12,20},{16,8},{20,28},{24,16},{28,36},{32,24}... | collective-permute-start | bytes 786440 | tf_op jit(solution)/shard_map/ppermute | solution.py:368
  65.5 9.7 %collective-permute-start.6 = (f32[8,16,512]{2,1,0:T(8,128)}, f32[8,16,512]{2,1,0:T(8,128)S(1)}, u32[]{:S(2)}, u32[]{:S(2)}) collective-permute-start(f32[8,16,512]{2,1,0:T(8,128)} %collective-permute-done.5.refs_3_), channel_id=1, source_target_pairs={{0,8},{4,60},{8,16},{12,4},{16,24},{20,12},{24,32},{28,20},{32,40}... | collective-permute-start | bytes 786440 | tf_op jit(solution)/shard_map/ppermute | solution.py:366
  70.1 5.9 %copy-start.6 = (f32[16,16,512]{2,1,0:T(8,128)}, f32[16,16,512]{2,1,0:T(8,128)S(1)}, u32[]{:S(2)}) copy-start(f32[16,16,512]{2,1,0:T(8,128)S(1)} %collective-permute-done.19.refs_11_) | copy-start | bytes 1572868
  74.5 0.7 copy-start.12
  75.2 0.7 copy-start.13
  76.0 0.8 copy-start.7
  82.2 17.4 %collective-permute-start.20 = (f32[24,32,512]{2,1,0:T(8,128)}, f32[24,32,512]{2,1,0:T(8,128)S(1)}, u32[]{:S(2)}, u32[]{:S(2)}) collective-permute-start(f32[24,32,512]{2,1,0:T(8,128)} %get-tuple-element.25), channel_id=1, source_target_pairs={{0,4},{4,0},{8,12},{12,8},{16,20},{20,16},{24,28},{28,24},{32,36},... | collective-permute-start | bytes 4718600 | tf_op jit(solution)/shard_map/ppermute | solution.py:403
  101.3 31.2 %copy-start.1 = (f32[24,32,512]{2,1,0:T(8,128)}, f32[24,32,512]{2,1,0:T(8,128)S(1)}, u32[]{:S(2)}) copy-start(f32[24,32,512]{2,1,0:T(8,128)S(1)} %broadcast_select_fusion.p0) | copy-start | bytes 4718596
  101.3 31.2 %collective-permute-start.21 = (f32[24,32,512]{2,1,0:T(8,128)S(1)}, f32[24,32,512]{2,1,0:T(8,128)S(1)}, u32[]{:S(2)}, u32[]{:S(2)}) collective-permute-start(f32[24,32,512]{2,1,0:T(8,128)S(1)} %broadcast_select_fusion.p0), channel_id=1, source_target_pairs={{0,1},{1,2},{2,3},{3,0},{4,7},{5,4},{6,5},{7,6},{8,9},{9,10},{10,1... | collective-permute-start | bytes 4718600 | tf_op jit(solution)/shard_map/ppermute | solution.py:406
  132.5 36.1 %collective-permute-start.22 = (f32[24,32,512]{2,1,0:T(8,128)S(1)}, f32[24,32,512]{2,1,0:T(8,128)}, u32[]{:S(2)}, u32[]{:S(2)}) collective-permute-start(f32[24,32,512]{2,1,0:T(8,128)S(1)} %broadcast_select_fusion.p0), channel_id=1, source_target_pairs={{0,3},{1,0},{2,1},{3,2},{4,5},{5,6},{6,7},{7,4},{8,11},{9,8},{10,9... | collective-permute-start | bytes 4718600 | tf_op jit(solution)/shard_map/ppermute | solution.py:407
  132.5 13.4 %copy-start.2 = (f32[24,32,512]{2,1,0:T(8,128)}, f32[24,32,512]{2,1,0:T(8,128)S(1)}, u32[]{:S(2)}) copy-start(f32[24,32,512]{2,1,0:T(8,128)S(1)} %collective-permute-done.21.p1) | copy-start | bytes 4718596
  132.5 36.1 %collective-permute-start.23 = (f32[24,32,512]{2,1,0:T(8,128)S(1)}, f32[24,32,512]{2,1,0:T(8,128)}, u32[]{:S(2)}, u32[]{:S(2)}) collective-permute-start(f32[24,32,512]{2,1,0:T(8,128)S(1)} %collective-permute-done.21.p1), channel_id=1, source_target_pairs={{0,1},{1,2},{2,3},{3,0},{4,7},{5,4},{6,5},{7,6},{8,9},{9,10},{10,1... | collective-permute-start | bytes 4718600 | tf_op jit(solution)/shard_map/ppermute | solution.py:408
  135.2 13.3 %copy-start.14 = (s32[20,2]{0,1:T(2,128)S(1)}, s32[20,2]{0,1:T(2,128)}, u32[]{:S(2)}) copy-start(s32[20,2]{0,1:T(2,128)} %param.13) | copy-start | bytes 484
Sparse Core Ops, SparseCore 0:
  10.8 152.4 all-gather.1

commit v2 on v1

--- a/solution.py
+++ b/solution.py
@@ -249,44 +249,102 @@
     )(place, *zy, *yz)
 
 
-def update_kernel(info, tile, full_high, full_low, p0, p1, p2, p3, table, out, stage, lh, ll, rh, rl, sems):
+def left_kernel(info, p0, p1, p2, p3, full_high, full_low, high, low):
+    step, rows, _ = p0.shape
+    first = pl.program_id(0) * step
+    parts = (p0, p1, p2, p3)
+    pieces = [jnp.where(info[4 + first + g] > 0, p[g], 0.0) for p in parts for g in range(step)]
+    xh, xl = split(jnp.concatenate(pieces, axis=0))
+    yh, yl = split(dot3(xh, xl, full_high[...], full_low[...]))
+    for i in range(len(parts)):
+        at = pl.ds(pl.multiple_of(info[i] * rows, rows), rows)
+        for g in range(step):
+            here = slice((i * step + g) * rows, (i * step + g + 1) * rows)
+            high[g, at, :] = yh[here]
+            low[g, at, :] = yl[here]
+
+
+def left_rows(parts, full_high, full_low, quarters, valid):
+    count, rows, n = parts[0].shape
+    half = count // 2
+    step = 2
+    head = rows * len(parts)
+    info = jnp.concatenate([jnp.stack(quarters), valid[:half]]).astype(jnp.int32)
+    shape = jax.ShapeDtypeStruct((half, head, n), BF)
+    whole = pl.BlockSpec((n, n), lambda i, s: (0, 0))
+    target = pl.BlockSpec((step, head, n), lambda i, s: (i, 0, 0))
+    return pl.pallas_call(
+        left_kernel,
+        out_shape=(shape, shape),
+        grid_spec=pltpu.PrefetchScalarGridSpec(
+            num_scalar_prefetch=1,
+            grid=(half // step,),
+            in_specs=[pl.BlockSpec((step, rows, n), lambda i, s: (i, 0, 0))] * len(parts) + [whole, whole],
+            out_specs=(target, target),
+        ),
+        cost_estimate=cost(half * head * n * n * 6, half * head * n * 8),
+        name="left_rows",
+    )(info, *parts, full_high, full_low)
+
+
+def update_kernel(info, tile, full_high, full_low, gh, gl, p0, p1, p2, p3, table, out, near, side, lh, ll, rh, rl, sems):
     k = pl.program_id(0)
-    count, b, _ = stage.shape
-    half = count // 2
+    half, b, _ = side.shape
+    tail = near.shape[1]
+    head = b - tail
     rows = p0.shape[1]
-    tail = table.shape[1]
 
     @pl.when(k == 0)
     def _():
         parts = [
-            pltpu.make_async_copy(p, stage.at[:, pl.ds(pl.multiple_of(info[3, i] * rows, rows), rows), :], sems.at[count + i])
+            pltpu.make_async_copy(
+                p.at[pl.ds(half, half)],
+                side.at[:, pl.ds(pl.multiple_of(info[3, i] * rows, rows), rows), :],
+                sems.at[2 * half + i],
+            )
             for i, p in enumerate((p0, p1, p2, p3))
         ]
+        ready = [
+            pltpu.make_async_copy(gh, lh.at[:, pl.ds(0, head), :], sems.at[2 * half + 4]),
+            pltpu.make_async_copy(gl, ll.at[:, pl.ds(0, head), :], sems.at[2 * half + 5]),
+        ]
+
+        def rest(g):
+            return (
+                pltpu.make_async_copy(table.at[info[4, g]], near.at[g], sems.at[g]),
+                pltpu.make_async_copy(table.at[info[4, half + g]], side.at[g, pl.ds(head, tail), :], sems.at[half + g]),
+            )
+
         for c in parts:
             c.start()
 
-        def rest(g):
-            return pltpu.make_async_copy(table.at[info[4, g]], stage.at[g, pl.ds(b - tail, tail), :], sems.at[g])
-
         @pl.loop(0, half)
         def _(g):
-            rest(g).start()
-            rest(g + half).start()
-
+            for c in rest(g):
+                c.start()
+
+        for c in ready:
+            c.start()
         for c in parts:
             c.wait()
 
-        @pl.loop(0, half)
-        def _(g):
-            rest(g).wait()
-            rest(g + half).wait()
-            xh, xl = split(jnp.where(info[5, g] > 0, stage[g], 0.0))
+        @pl.loop(0, half // 2)
+        def _(i):
+            pair = (2 * i, 2 * i + 1)
+            for g in pair:
+                for c in rest(g):
+                    c.wait()
+            xh, xl = split(jnp.concatenate([jnp.where(info[5, g] > 0, near[g], 0.0) for g in pair], axis=0))
             yh, yl = split(dot3(xh, xl, full_high[...], full_low[...]))
-            lh[g] = yh
-            ll[g] = yl
-            xh, xl = split(jnp.where(info[5, g + half] > 0, stage[g + half], 0.0))
-            rh[g] = xh
-            rl[g] = xl
+            for at, g in enumerate(pair):
+                lh[g, pl.ds(head, tail), :] = yh[at * tail : (at + 1) * tail]
+                ll[g, pl.ds(head, tail), :] = yl[at * tail : (at + 1) * tail]
+                xh, xl = split(jnp.where(info[5, half + g] > 0, side[g], 0.0))
+                rh[g] = xh
+                rl[g] = xl
+
+        for c in ready:
+            c.wait()
 
     @pl.loop(0, tile.shape[0], unroll=2)
     def _(t):
@@ -296,7 +354,7 @@
         out[t] = tile[t] - jnp.where(info[2, slot] > 0, product, 0.0)
 
 
-def update_tiles(tiles, full_high, full_low, parts, quarters, table, slots, valid, pairs):
+def update_tiles(tiles, full_high, full_low, left, parts, quarters, table, slots, valid, pairs):
     total, b, _ = tiles.shape
     count = slots.shape[0]
     half = count // 2
@@ -324,16 +382,16 @@
         grid_spec=pltpu.PrefetchScalarGridSpec(
             num_scalar_prefetch=1,
             grid=(total // block,),
-            in_specs=[tspec, whole, whole] + [anywhere] * 5,
+            in_specs=[tspec, whole, whole] + [anywhere] * 7,
             out_specs=tspec,
-            scratch_shapes=[pltpu.VMEM((count, b, n), F32)]
+            scratch_shapes=[pltpu.VMEM((half, table.shape[1], n), F32), pltpu.VMEM((half, b, n), F32)]
             + [operand] * 4
-            + [pltpu.SemaphoreType.DMA((count + 4,))],
+            + [pltpu.SemaphoreType.DMA((count + 6,))],
         ),
         compiler_params=pltpu.CompilerParams(vmem_limit_bytes=58 * 2**20),
         cost_estimate=cost(total * b * b * n * 6 + half * b * n * n * 6, total * b * 8 * b + count * b * n * 4),
         name="update_tiles",
-    )(info, tiles, full_high, full_low, *parts, table)
+    )(info, tiles, full_high, full_low, *left, *parts, table)
 
 
 def turned(core, step):
@@ -411,7 +469,8 @@
     high, low, full_high, full_low, diag = factorize(pivot_blocks, coupling)
     factors = own_factors(panel_rows, high, low, diag, own_ids < NB)
     parts = (mine, one, other, far)
-    updated = update_tiles(trailing_tiles, full_high, full_low, parts, quarters, gathered, slots, valid, tile_pairs)
+    left = left_rows(parts, full_high, full_low, quarters, valid)
+    updated = update_tiles(trailing_tiles, full_high, full_low, left, parts, quarters, gathered, slots, valid, tile_pairs)
     return (updated, factors, diag.reshape(2, b))
 
 

time: 198 us -> 210 us (1.061)
  waiting for transfers between devices: 48.9 us -> 55.4 us
  Pallas kernels: 69.9 us -> 73.5 us
    ppermute x1, waiting for transfers between devices: 14.9 us -> 25.3 us  [per_device(): other = lax.ppermute(mine, both, back)]
    pallas_call x0 -> x1, Pallas kernels: none -> 7.98 us  [left_rows(): pl.pallas_call(left_kernel, out_shape=(shape, shape), grid_spec=pltpu.Pre...]
    pallas_call x1, Pallas kernels: 21.7 us -> 17.2 us  [update_tiles(): pl.pallas_call(update_kernel, out_shape=jax.ShapeDtypeStruct(tiles.shape,...]
    ppermute x1, waiting for transfers between devices: 3.96 us -> 0.01 us  [per_device(): lax.ppermute(theirs, 'tiles', swap)]
    unnamed x40 -> x44, local copies, waits for them, and re-layouts: 3.29 us -> 4.42 us
  transfers between devices with their start and end apart: 25 -> 25, of which waited for: 9 -> 8; matrix products, arithmetic and copies ran while one was open for 4% -> 4% of each run, Pallas kernels for 24% -> 27%
where the time goes in v2:
time: 210 us; the launch traced here: 209 us
  Pallas kernels  73.5 us (35%)
  waiting for transfers between devices  55.4 us (26%)
  starting transfers between devices  51.9 us (25%)
  between operations  14.4 us (7%)
  local copies, waits for them, and re-layouts  8.9 us (4%)
  other arithmetic  4.73 us (2%)
    ppermute x12, starting transfers between devices, ring(): near.append(lax.ppermute(near[-1], 'tiles', ahead))  29.1 us
    ppermute x1, waiting for transfers between devices, per_device(): other = lax.ppermute(mine, both, back)  25.3 us
    pallas_call x2, Pallas kernels, factorize(): pl.pallas_call(functools.partial(middle_kernel, at), out_shape=(full, dsh...  18.1 us
    ppermute x8, waiting for transfers between devices, ring(): far.append(lax.ppermute(far[-1], 'tiles', back))  17.5 us
    pallas_call x1, Pallas kernels, update_tiles(): pl.pallas_call(update_kernel, out_shape=jax.ShapeDtypeStruct(tiles.shape,...  17.2 us
    ppermute x1, starting transfers between devices, per_device(): lax.ppermute(theirs, 'tiles', swap)  13.4 us
    ppermute x12, waiting for transfers between devices, ring(): near.append(lax.ppermute(near[-1], 'tiles', ahead))  12.6 us
    pallas_call x1, Pallas kernels, factorize(): pl.pallas_call(functools.partial(last_kernel, 6), out_shape=(half, half,...  10.7 us
  transfers between devices with their start and end apart: 25, of which 8 were waited for; matrix products, arithmetic and copies ran while one was open for 4% of the time, Pallas kernels for 27%

profile of v2, /device:TPU:1, one launch (start us, length us, event | category | flops | bytes accessed | tf_op | source)
XLA Modules:
  0.0 208.8 jit_solution(18445274013698376210)
XLA Ops:
  7.2 0.0 copy-start
  7.2 0.0 all-gather.2.cloned.1.call-start
  7.2 1.9 slice.28
  9.1 0.0 all-gather.2.cloned.1.call-update
  9.2 0.9 constant_dynamic-update-slice_fusion.7
  10.1 2.5 %collective-permute-start.14 = (f32[2,16,512]{2,1,0:T(8,128)S(1)}, f32[2,16,512]{2,1,0:T(8,128)S(1)}, u32[]{:S(2)}, u32[]{:S(2)}) collective-permute-start(f32[2,16,512]{2,1,0:T(8,128)S(1)} %get-tuple-element.34), channel_id=1, source_target_pairs={{0,56},{4,12},{8,0},{12,20},{16,8},{20,28},{24,16},{28,36},{32,24}... | collective-permute-start | bytes 196616 | tf_op jit(solution)/shard_map/ppermute | solution.py:426
  12.6 4.0 %collective-permute-start.10 = (f32[2,16,512]{2,1,0:T(8,128)S(1)}, f32[2,16,512]{2,1,0:T(8,128)S(1)}, u32[]{:S(2)}, u32[]{:S(2)}) collective-permute-start(f32[2,16,512]{2,1,0:T(8,128)S(1)} %get-tuple-element.34), channel_id=1, source_target_pairs={{0,8},{4,60},{8,16},{12,4},{16,24},{20,12},{24,32},{28,20},{32,40}... | collective-permute-start | bytes 196616 | tf_op jit(solution)/shard_map/ppermute | solution.py:424
  16.6 2.7 %collective-permute-start = (f32[2,16,512]{2,1,0:T(8,128)S(1)}, f32[2,16,512]{2,1,0:T(8,128)S(1)}, u32[]{:S(2)}, u32[]{:S(2)}) collective-permute-start(f32[2,16,512]{2,1,0:T(8,128)S(1)} %get-tuple-element.37), channel_id=1, source_target_pairs={{0,64},{4,196},{8,72},{12,204},{16,80},{20,212},{24,88},{28,220},{... | collective-permute-start | bytes 196616 | tf_op jit(solution)/shard_map/ppermute | solution.py:424
  19.4 0.0 collective-permute-start.2
  19.4 0.0 collective-permute-done.14
  19.4 0.0 collective-permute-done.10
  19.4 2.7 %collective-permute-start.11 = (f32[2,16,512]{2,1,0:T(8,128)S(1)}, f32[2,16,512]{2,1,0:T(8,128)S(1)}, u32[]{:S(2)}, u32[]{:S(2)}) collective-permute-start(f32[2,16,512]{2,1,0:T(8,128)S(1)} %collective-permute-done.10), channel_id=1, source_target_pairs={{0,8},{4,60},{8,16},{12,4},{16,24},{20,12},{24,32},{28,20},{32,40}... | collective-permute-start | bytes 196616 | tf_op jit(solution)/shard_map/ppermute | solution.py:424
  22.0 0.0 collective-permute-done
  22.0 2.7 %collective-permute-start.1 = (f32[2,16,512]{2,1,0:T(8,128)S(1)}, f32[2,16,512]{2,1,0:T(8,128)S(1)}, u32[]{:S(2)}, u32[]{:S(2)}) collective-permute-start(f32[2,16,512]{2,1,0:T(8,128)S(1)} %collective-permute-done), channel_id=1, source_target_pairs={{0,64},{4,196},{8,72},{12,204},{16,80},{20,212},{24,88},{28,220},{... | collective-permute-start | bytes 196616 | tf_op jit(solution)/shard_map/ppermute | solution.py:424
  24.7 0.0 collective-permute-done.2
  24.7 1.3 collective-permute-done.1
  26.1 0.4 collective-permute-start.3
  26.5 1.1 collective-permute-start.16
  27.6 1.5 collective-permute-start.12
  29.2 7.3 %collective-permute-done.12 = f32[2,16,512]{2,1,0:T(8,128)S(1)} collective-permute-done((f32[2,16,512]{2,1,0:T(8,128)S(1)}, f32[2,16,512]{2,1,0:T(8,128)S(1)}, u32[]{:S(2)}, u32[]{:S(2)}) %collective-permute-start.12) | collective-permute-done | bytes 65568 | tf_op jit(solution)/shard_map/ppermute | solution.py:424
  36.5 0.4 collective-permute-start.13
  36.9 4.0 %collective-permute-done.13 = f32[2,16,512]{2,1,0:T(8,128)S(1)} collective-permute-done((f32[2,16,512]{2,1,0:T(8,128)S(1)}, f32[2,16,512]{2,1,0:T(8,128)S(1)}, u32[]{:S(2)}, u32[]{:S(2)}) %collective-permute-start.13) | collective-permute-done | bytes 65568 | tf_op jit(solution)/shard_map/ppermute | solution.py:424
  40.9 0.0 copy-start.6
  40.9 4.2 %collective-permute-start.17 = (f32[16,16,512]{2,1,0:T(8,128)S(1)}, f32[16,16,512]{2,1,0:T(8,128)S(1)}, u32[]{:S(2)}, u32[]{:S(2)}) collective-permute-start(f32[16,16,512]{2,1,0:T(8,128)S(1)} %constant_dynamic-update-slice_fusion.refs_8_), channel_id=1, source_target_pairs={{0,64},{4,196},{8,72},{12,204},{16,80},{20,212},{24,88},{28,220},{... | collective-permute-start | bytes 1572872 | tf_op jit(solution)/shard_map/ppermute | solution.py:424
  45.1 2.7 %collective-permute-start.4 = (f32[8,16,512]{2,1,0:T(8,128)S(1)}, f32[8,16,512]{2,1,0:T(8,128)S(1)}, u32[]{:S(2)}, u32[]{:S(2)}) collective-permute-start(f32[8,16,512]{2,1,0:T(8,128)S(1)} %collective-permute-done.3.refs_1_), channel_id=1, source_target_pairs={{0,8},{4,60},{8,16},{12,4},{16,24},{20,12},{24,32},{28,20},{32,40}... | collective-permute-start | bytes 786440 | tf_op jit(solution)/shard_map/ppermute | solution.py:424
  47.8 0.1 constant_dynamic-slice_fusion.3
  47.8 0.1 copy.20
  47.9 9.6 %collective-permute-done.7.refs_7_ = f32[8,16,512]{2,1,0:T(8,128)S(1)} collective-permute-done((f32[8,16,512]{2,1,0:T(8,128)S(1)}, f32[8,16,512]{2,1,0:T(8,128)S(1)}, u32[]{:S(2)}, u32[]{:S(2)}) %collective-permute-start.7) | collective-permute-done | bytes 262176 | tf_op jit(solution)/shard_map/ppermute | solution.py:426
  57.6 2.7 %collective-permute-start.5 = (f32[8,16,512]{2,1,0:T(8,128)S(1)}, f32[8,16,512]{2,1,0:T(8,128)}, u32[]{:S(2)}, u32[]{:S(2)}) collective-permute-start(f32[8,16,512]{2,1,0:T(8,128)S(1)} %collective-permute-done.4.refs_2_), channel_id=1, source_target_pairs={{0,8},{4,60},{8,16},{12,4},{16,24},{20,12},{24,32},{28,20},{32,40}... | collective-permute-start | bytes 786440 | tf_op jit(solution)/shard_map/ppermute | solution.py:424
  60.3 0.2 select_reduce_fusion
  60.6 0.1 collective-permute-start.19
  60.7 2.6 %collective-permute-start.18 = (f32[16,16,512]{2,1,0:T(8,128)S(1)}, f32[16,16,512]{2,1,0:T(8,128)S(1)}, u32[]{:S(2)}, u32[]{:S(2)}) collective-permute-start(f32[16,16,512]{2,1,0:T(8,128)S(1)} %collective-permute-done.17.refs_9_), channel_id=1, source_target_pairs={{0,64},{4,196},{8,72},{12,204},{16,80},{20,212},{24,88},{28,220},{... | collective-permute-start | bytes 1572872 | tf_op jit(solution)/shard_map/ppermute | solution.py:424
  63.3 1.6 collective-permute-done.8.refs_6_
  65.0 0.2 collective-permute-start.9
  65.2 2.4 %collective-permute-start.6 = (f32[8,16,512]{2,1,0:T(8,128)}, f32[8,16,512]{2,1,0:T(8,128)S(1)}, u32[]{:S(2)}, u32[]{:S(2)}) collective-permute-start(f32[8,16,512]{2,1,0:T(8,128)} %collective-permute-done.5.refs_3_), channel_id=1, source_target_pairs={{0,8},{4,60},{8,16},{12,4},{16,24},{20,12},{24,32},{28,20},{32,40}... | collective-permute-start | bytes 786440 | tf_op jit(solution)/shard_map/ppermute | solution.py:424
  67.7 0.6 pad_add_fusion.place
  68.3 2.0 collective-permute-done.19.refs_11_
  70.3 4.2 %collective-permute-done.9.refs_5_ = f32[8,16,512]{2,1,0:T(8,128)S(1)} collective-permute-done((f32[8,16,512]{2,1,0:T(8,128)S(1)}, f32[8,16,512]{2,1,0:T(8,128)S(1)}, u32[]{:S(2)}, u32[]{:S(2)}) %collective-permute-start.9) | collective-permute-done | bytes 262176 | tf_op jit(solution)/shard_map/ppermute | solution.py:426
  74.5 0.7 copy-done.14
  75.2 0.7 copy-done.15
  76.0 0.8 copy-done.9
  76.8 5.4 %pick.1 = (f32[24,32,512]{2,1,0:T(8,128)}, f32[24,32,512]{2,1,0:T(8,128)}) custom-call(s32[2,3,24]{2,1,0:T(4,128)} %pad_add_fusion.place, f32[8,16,512]{2,1,0:T(8,128)} %copy-done.5, f32[8,16,512]{2,1,0:T(8,128)} %copy-done.10, f32[8,16,512]{2,1,0:T(8,128)} %copy-done.12, f32[8,16,512]{2,1,0:T(8,128)} %collective-permute-done.5.refs_3_, ...), custom_call_target="tpu_custom_call" | custom-call | bytes 6291456 | tf_op jit(solution)/shard_map/pick/pallas_call | solution.py:237
  82.2 13.4 %collective-permute-start.20 = (f32[24,32,512]{2,1,0:T(8,128)}, f32[24,32,512]{2,1,0:T(8,128)S(1)}, u32[]{:S(2)}, u32[]{:S(2)}) collective-permute-start(f32[24,32,512]{2,1,0:T(8,128)} %get-tuple-element.27), channel_id=1, source_target_pairs={{0,4},{4,0},{8,12},{12,8},{16,20},{20,16},{24,28},{28,24},{32,36},... | collective-permute-start | bytes 4718600 | tf_op jit(solution)/shard_map/ppermute | solution.py:461
  95.6 10.2 %panels0.1 = (f32[512,512]{1,0:T(8,128)}, f32[1,128]{1,0:T(1,128)}) custom-call(f32[2,256,256]{2,1,0:T(8,128)} %pivot.1, f32[256,256]{1,0:T(8,128)} %coupling.1), custom_call_target="tpu_custom_call" | custom-call | flops 6000000000 | bytes 2097152 | tf_op jit(solution)/shard_map/panels0/pallas_call | solution.py:142
  105.9 1.2 copy-done.4
  107.0 1.9 broadcast_select_fusion.p0
  108.9 2.7 %collective-permute-start.21 = (f32[24,32,512]{2,1,0:T(8,128)S(1)}, f32[24,32,512]{2,1,0:T(8,128)S(1)}, u32[]{:S(2)}, u32[]{:S(2)}) collective-permute-start(f32[24,32,512]{2,1,0:T(8,128)S(1)} %broadcast_select_fusion.p0), channel_id=1, source_target_pairs={{0,1},{1,2},{2,3},{3,0},{4,7},{5,4},{6,5},{7,6},{8,9},{9,10},{10,1... | collective-permute-start | bytes 4718600 | tf_op jit(solution)/shard_map/ppermute | solution.py:464
  111.6 9.4 %shard_map.94 = (f32[512,512]{1,0:T(8,128)}, f32[1,128]{1,0:T(1,128)}) custom-call(f32[512,512]{1,0:T(8,128)} %get-tuple-element.18.before), custom_call_target="tpu_custom_call" | custom-call | flops 6000000000 | bytes 2097152 | tf_op jit(solution)/shard_map/pallas_call | solution.py:147
  121.1 8.6 %shard_map.95 = (f32[512,512]{1,0:T(8,128)}, f32[1,128]{1,0:T(1,128)}) custom-call(f32[512,512]{1,0:T(8,128)} %get-tuple-element.19.before), custom_call_target="tpu_custom_call" | custom-call | flops 6000000000 | bytes 2097152 | tf_op jit(solution)/shard_map/pallas_call | solution.py:147
  129.7 10.7 %panels6.1 = (bf16[512,512]{1,0:T(8,128)(2,1)}, bf16[512,512]{1,0:T(8,128)(2,1)}, bf16[512,512]{1,0:T(8,128)(2,1)}, bf16[512,512]{1,0:T(8,128)(2,1)}, f32[1,512]{1,0:T(1,128)}) custom-call(f32[512,512]{1,0:T(8,128)} %get-tuple-element.20.before, f32[1,128]{1,0:T(1,128)} %get-tuple-element.21.d0, f32[1,128]{1,0:T(1,128)} %get-tuple-element.22.d1, ...), custom_call_target="tpu_custom_call" | custom-call | flops 6000000000 | bytes 2097152 | tf_op jit(solution)/shard_map/panels6/pallas_call | solution.py:151
  140.5 2.7 %collective-permute-start.23 = (f32[24,32,512]{2,1,0:T(8,128)S(1)}, f32[24,32,512]{2,1,0:T(8,128)}, u32[]{:S(2)}, u32[]{:S(2)}) collective-permute-start(f32[24,32,512]{2,1,0:T(8,128)S(1)} %collective-permute-done.21.p1), channel_id=1, source_target_pairs={{0,1},{1,2},{2,3},{3,0},{4,7},{5,4},{6,5},{7,6},{8,9},{9,10},{10,1... | collective-permute-start | bytes 4718600 | tf_op jit(solution)/shard_map/ppermute | solution.py:466
  143.1 0.1 constant_dynamic-slice_fusion.2
  143.2 0.1 copy.25
  143.3 0.5 broadcast.173
  143.8 1.3 reduce.3
  145.1 0.6 reshape.67
  145.7 0.6 concatenate.9.info
  146.3 0.1 pad_add_fusion.1
  146.4 0.6 stack.61.info
  147.0 0.6 compare_convert_fusion.keep
  147.6 3.8 %own_factors.1 = f32[2,256,512]{2,1,0:T(8,128)} custom-call(s32[2]{0:T(128)} %compare_convert_fusion.keep, f32[2,256,512]{2,1,0:T(8,128)} %x.9, bf16[512,512]{1,0:T(8,128)(2,1)} %get-tuple-element.30.high, bf16[512,512]{1,0:T(8,128)(2,1)} %get-tuple-element.31.low, f32[1,512]{1,0:T(1,128)} %get-tuple-element.32.diag), custom_call_target="tpu_custom_call" | custom-call | flops 805306368 | bytes 2097152 | tf_op jit(solution)/shard_map/own_factors/pallas_call | solution.py:177
  151.5 25.3 %collective-permute-done.22.p2 = f32[24,32,512]{2,1,0:T(8,128)} collective-permute-done((f32[24,32,512]{2,1,0:T(8,128)S(1)}, f32[24,32,512]{2,1,0:T(8,128)}, u32[]{:S(2)}, u32[]{:S(2)}) %collective-permute-start.22) | collective-permute-done | bytes 1572896 | tf_op jit(solution)/shard_map/ppermute | solution.py:465
  176.8 8.0 %left_rows.1 = (bf16[12,128,512]{2,1,0:T(8,128)(2,1)}, bf16[12,128,512]{2,1,0:T(8,128)(2,1)}) custom-call(s32[16]{0:T(128)} %concatenate.9.info, f32[24,32,512]{2,1,0:T(8,128)} %copy-done.1, f32[24,32,512]{2,1,0:T(8,128)} %copy-done.2, f32[24,32,512]{2,1,0:T(8,128)} %collective-permute-done.22.p2, f32[24,32,512]{2,1,0:T(8,128)} %collective-permute-done.23.p3, ...), custom_call_target="tpu_custom_call" | custom-call | flops 2415919104 | bytes 6291456 | tf_op jit(solution)/shard_map/left_rows/pallas_call | solution.py:276
  184.7 17.2 %update_tiles.1 = f32[20,256,256]{2,1,0:T(8,128)} custom-call(s32[6,24]{1,0:T(8,128)} %stack.61.info, f32[20,256,256]{2,1,0:T(8,128)} %tile.1, bf16[512,512]{1,0:T(8,128)(2,1)} %get-tuple-element.24.full_high, bf16[512,512]{1,0:T(8,128)(2,1)} %get-tuple-element.25.full_low, bf16[12,128,512]{2,1,0:T(8,128)(2,1)} %get-tuple-element.28.gh, ...), custom_call_target="tpu_custom_call" | custom-call | flops 8858370048 | bytes 23068672 | tf_op jit(solution)/shard_map/update_tiles/pallas_call | solution.py:379
  (67 shorter events, 0.3 us)
Async XLA Ops:
  7.2 40.6 %copy-start = (s32[64,24]{0,1:T(8,128)S(1)}, s32[64,24]{0,1:T(8,128)}, u32[]{:S(2)}) copy-start(s32[64,24]{0,1:T(8,128)} %param.12) | copy-start | bytes 18436
  7.2 53.1 %copy-start.17 = (s32[128]{0:T(128)S(1)}, s32[128]{0:T(128)}, u32[]{:S(2)}) copy-start(s32[128]{0:T(128)} %param.11) | copy-start | bytes 1540
  7.2 177.5 %all-gather.2.cloned.1.call-start = ((), (), s32[]{:S(2)}) async-start(), calls=%async_computation | async-start | bytes 34078720 | tf_op jit(solution)/shard_map/all_gather | solution.py:439
  10.1 9.3 %collective-permute-start.14 = (f32[2,16,512]{2,1,0:T(8,128)S(1)}, f32[2,16,512]{2,1,0:T(8,128)S(1)}, u32[]{:S(2)}, u32[]{:S(2)}) collective-permute-start(f32[2,16,512]{2,1,0:T(8,128)S(1)} %get-tuple-element.34), channel_id=1, source_target_pairs={{0,56},{4,12},{8,0},{12,20},{16,8},{20,28},{24,16},{28,36},{32,24}... | collective-permute-start | bytes 196616 | tf_op jit(solution)/shard_map/ppermute | solution.py:426
  12.6 6.8 %collective-permute-start.10 = (f32[2,16,512]{2,1,0:T(8,128)S(1)}, f32[2,16,512]{2,1,0:T(8,128)S(1)}, u32[]{:S(2)}, u32[]{:S(2)}) collective-permute-start(f32[2,16,512]{2,1,0:T(8,128)S(1)} %get-tuple-element.34), channel_id=1, source_target_pairs={{0,8},{4,60},{8,16},{12,4},{16,24},{20,12},{24,32},{28,20},{32,40}... | collective-permute-start | bytes 196616 | tf_op jit(solution)/shard_map/ppermute | solution.py:424
  16.6 5.4 %collective-permute-start = (f32[2,16,512]{2,1,0:T(8,128)S(1)}, f32[2,16,512]{2,1,0:T(8,128)S(1)}, u32[]{:S(2)}, u32[]{:S(2)}) collective-permute-start(f32[2,16,512]{2,1,0:T(8,128)S(1)} %get-tuple-element.37), channel_id=1, source_target_pairs={{0,64},{4,196},{8,72},{12,204},{16,80},{20,212},{24,88},{28,220},{... | collective-permute-start | bytes 196616 | tf_op jit(solution)/shard_map/ppermute | solution.py:424
  19.4 5.4 %collective-permute-start.2 = (f32[2,16,512]{2,1,0:T(8,128)S(1)}, f32[2,16,512]{2,1,0:T(8,128)S(1)}, u32[]{:S(2)}, u32[]{:S(2)}) collective-permute-start(f32[2,16,512]{2,1,0:T(8,128)S(1)} %get-tuple-element.37), channel_id=1, source_target_pairs={{0,192},{4,68},{8,200},{12,76},{16,208},{20,84},{24,216},{28,92},{... | collective-permute-start | bytes 196616 | tf_op jit(solution)/shard_map/ppermute | solution.py:426
  19.4 7.1 %collective-permute-start.15 = (f32[2,16,512]{2,1,0:T(8,128)S(1)}, f32[2,16,512]{2,1,0:T(8,128)S(1)}, u32[]{:S(2)}, u32[]{:S(2)}) collective-permute-start(f32[2,16,512]{2,1,0:T(8,128)S(1)} %collective-permute-done.14), channel_id=1, source_target_pairs={{0,56},{4,12},{8,0},{12,20},{16,8},{20,28},{24,16},{28,36},{32,24}... | collective-permute-start | bytes 196616 | tf_op jit(solution)/shard_map/ppermute | solution.py:426
  19.4 8.3 %collective-permute-start.11 = (f32[2,16,512]{2,1,0:T(8,128)S(1)}, f32[2,16,512]{2,1,0:T(8,128)S(1)}, u32[]{:S(2)}, u32[]{:S(2)}) collective-permute-start(f32[2,16,512]{2,1,0:T(8,128)S(1)} %collective-permute-done.10), channel_id=1, source_target_pairs={{0,8},{4,60},{8,16},{12,4},{16,24},{20,12},{24,32},{28,20},{32,40}... | collective-permute-start | bytes 196616 | tf_op jit(solution)/shard_map/ppermute | solution.py:424
  22.0 4.0 %collective-permute-start.1 = (f32[2,16,512]{2,1,0:T(8,128)S(1)}, f32[2,16,512]{2,1,0:T(8,128)S(1)}, u32[]{:S(2)}, u32[]{:S(2)}) collective-permute-start(f32[2,16,512]{2,1,0:T(8,128)S(1)} %collective-permute-done), channel_id=1, source_target_pairs={{0,64},{4,196},{8,72},{12,204},{16,80},{20,212},{24,88},{28,220},{... | collective-permute-start | bytes 196616 | tf_op jit(solution)/shard_map/ppermute | solution.py:424
  26.1 49.9 %copy-start.5 = (f32[8,16,512]{2,1,0:T(8,128)}, f32[8,16,512]{2,1,0:T(8,128)S(1)}, u32[]{:S(2)}) copy-start(f32[8,16,512]{2,1,0:T(8,128)S(1)} %pad_maximum_fusion.refs_0_) | copy-start | bytes 786436
  26.1 19.0 %collective-permute-start.3 = (f32[8,16,512]{2,1,0:T(8,128)S(1)}, f32[8,16,512]{2,1,0:T(8,128)S(1)}, u32[]{:S(2)}, u32[]{:S(2)}) collective-permute-start(f32[8,16,512]{2,1,0:T(8,128)S(1)} %pad_maximum_fusion.refs_0_), channel_id=1, source_target_pairs={{0,8},{4,60},{8,16},{12,4},{16,24},{20,12},{24,32},{28,20},{32,40}... | collective-permute-start | bytes 786440 | tf_op jit(solution)/shard_map/ppermute | solution.py:424
  26.5 14.3 %collective-permute-start.16 = (f32[2,16,512]{2,1,0:T(8,128)S(1)}, f32[2,16,512]{2,1,0:T(8,128)S(1)}, u32[]{:S(2)}, u32[]{:S(2)}) collective-permute-start(f32[2,16,512]{2,1,0:T(8,128)S(1)} %collective-permute-done.15), channel_id=1, source_target_pairs={{0,56},{4,12},{8,0},{12,20},{16,8},{20,28},{24,16},{28,36},{32,24}... | collective-permute-start | bytes 196616 | tf_op jit(solution)/shard_map/ppermute | solution.py:426
  27.6 8.8 %collective-permute-start.12 = (f32[2,16,512]{2,1,0:T(8,128)S(1)}, f32[2,16,512]{2,1,0:T(8,128)S(1)}, u32[]{:S(2)}, u32[]{:S(2)}) collective-permute-start(f32[2,16,512]{2,1,0:T(8,128)S(1)} %collective-permute-done.11), channel_id=1, source_target_pairs={{0,8},{4,60},{8,16},{12,4},{16,24},{20,12},{24,32},{28,20},{32,40}... | collective-permute-start | bytes 196616 | tf_op jit(solution)/shard_map/ppermute | solution.py:424
  36.5 4.4 %collective-permute-start.13 = (f32[2,16,512]{2,1,0:T(8,128)S(1)}, f32[2,16,512]{2,1,0:T(8,128)S(1)}, u32[]{:S(2)}, u32[]{:S(2)}) collective-permute-start(f32[2,16,512]{2,1,0:T(8,128)S(1)} %collective-permute-done.12), channel_id=1, source_target_pairs={{0,8},{4,60},{8,16},{12,4},{16,24},{20,12},{24,32},{28,20},{32,40}... | collective-permute-start | bytes 196616 | tf_op jit(solution)/shard_map/ppermute | solution.py:424
  40.9 35.0 %copy-start.6 = (f32[16,16,512]{2,1,0:T(8,128)}, f32[16,16,512]{2,1,0:T(8,128)S(1)}, u32[]{:S(2)}) copy-start(f32[16,16,512]{2,1,0:T(8,128)S(1)} %constant_dynamic-update-slice_fusion.refs_8_) | copy-start | bytes 1572868
  40.9 19.7 %collective-permute-start.17 = (f32[16,16,512]{2,1,0:T(8,128)S(1)}, f32[16,16,512]{2,1,0:T(8,128)S(1)}, u32[]{:S(2)}, u32[]{:S(2)}) collective-permute-start(f32[16,16,512]{2,1,0:T(8,128)S(1)} %constant_dynamic-update-slice_fusion.refs_8_), channel_id=1, source_target_pairs={{0,64},{4,196},{8,72},{12,204},{16,80},{20,212},{24,88},{28,220},{... | collective-permute-start | bytes 1572872 | tf_op jit(solution)/shard_map/ppermute | solution.py:424
  45.1 12.4 %collective-permute-start.7 = (f32[8,16,512]{2,1,0:T(8,128)S(1)}, f32[8,16,512]{2,1,0:T(8,128)S(1)}, u32[]{:S(2)}, u32[]{:S(2)}) collective-permute-start(f32[8,16,512]{2,1,0:T(8,128)S(1)} %pad_maximum_fusion.refs_0_), channel_id=1, source_target_pairs={{0,56},{4,12},{8,0},{12,20},{16,8},{20,28},{24,16},{28,36},{32,24}... | collective-permute-start | bytes 786440 | tf_op jit(solution)/shard_map/ppermute | solution.py:426
  45.1 30.9 %copy-start.10 = (f32[8,16,512]{2,1,0:T(8,128)}, f32[8,16,512]{2,1,0:T(8,128)S(1)}, u32[]{:S(2)}) copy-start(f32[8,16,512]{2,1,0:T(8,128)S(1)} %collective-permute-done.3.refs_1_) | copy-start | bytes 786436
  45.1 12.4 %collective-permute-start.4 = (f32[8,16,512]{2,1,0:T(8,128)S(1)}, f32[8,16,512]{2,1,0:T(8,128)S(1)}, u32[]{:S(2)}, u32[]{:S(2)}) collective-permute-start(f32[8,16,512]{2,1,0:T(8,128)S(1)} %collective-permute-done.3.refs_1_), channel_id=1, source_target_pairs={{0,8},{4,60},{8,16},{12,4},{16,24},{20,12},{24,32},{28,20},{32,40}... | collective-permute-start | bytes 786440 | tf_op jit(solution)/shard_map/ppermute | solution.py:424
  57.5 18.4 %copy-start.11 = (f32[8,16,512]{2,1,0:T(8,128)}, f32[8,16,512]{2,1,0:T(8,128)S(1)}, u32[]{:S(2)}) copy-start(f32[8,16,512]{2,1,0:T(8,128)S(1)} %collective-permute-done.7.refs_7_) | copy-start | bytes 786436
  57.5 7.5 %collective-permute-start.8 = (f32[8,16,512]{2,1,0:T(8,128)S(1)}, f32[8,16,512]{2,1,0:T(8,128)S(1)}, u32[]{:S(2)}, u32[]{:S(2)}) collective-permute-start(f32[8,16,512]{2,1,0:T(8,128)S(1)} %collective-permute-done.7.refs_7_), channel_id=1, source_target_pairs={{0,56},{4,12},{8,0},{12,20},{16,8},{20,28},{24,16},{28,36},{32,24}... | collective-permute-start | bytes 786440 | tf_op jit(solution)/shard_map/ppermute | solution.py:426
  57.5 18.4 %copy-start.12 = (f32[8,16,512]{2,1,0:T(8,128)}, f32[8,16,512]{2,1,0:T(8,128)S(1)}, u32[]{:S(2)}) copy-start(f32[8,16,512]{2,1,0:T(8,128)S(1)} %collective-permute-done.4.refs_2_) | copy-start | bytes 786436
  57.6 7.7 %collective-permute-start.5 = (f32[8,16,512]{2,1,0:T(8,128)S(1)}, f32[8,16,512]{2,1,0:T(8,128)}, u32[]{:S(2)}, u32[]{:S(2)}) collective-permute-start(f32[8,16,512]{2,1,0:T(8,128)S(1)} %collective-permute-done.4.refs_2_), channel_id=1, source_target_pairs={{0,8},{4,60},{8,16},{12,4},{16,24},{20,12},{24,32},{28,20},{32,40}... | collective-permute-start | bytes 786440 | tf_op jit(solution)/shard_map/ppermute | solution.py:424
  60.6 9.7 %collective-permute-start.19 = (f32[16,16,512]{2,1,0:T(8,128)S(1)}, f32[16,16,512]{2,1,0:T(8,128)S(1)}, u32[]{:S(2)}, u32[]{:S(2)}) collective-permute-start(f32[16,16,512]{2,1,0:T(8,128)S(1)} %constant_dynamic-update-slice_fusion.refs_8_), channel_id=1, source_target_pairs={{0,192},{4,68},{8,200},{12,76},{16,208},{20,84},{24,216},{28,92},{... | collective-permute-start | bytes 1572872 | tf_op jit(solution)/shard_map/ppermute | solution.py:426
  60.7 15.3 %copy-start.7 = (f32[16,16,512]{2,1,0:T(8,128)}, f32[16,16,512]{2,1,0:T(8,128)S(1)}, u32[]{:S(2)}) copy-start(f32[16,16,512]{2,1,0:T(8,128)S(1)} %collective-permute-done.17.refs_9_) | copy-start | bytes 1572868
  60.7 15.3 %collective-permute-start.18 = (f32[16,16,512]{2,1,0:T(8,128)S(1)}, f32[16,16,512]{2,1,0:T(8,128)S(1)}, u32[]{:S(2)}, u32[]{:S(2)}) collective-permute-start(f32[16,16,512]{2,1,0:T(8,128)S(1)} %collective-permute-done.17.refs_9_), channel_id=1, source_target_pairs={{0,64},{4,196},{8,72},{12,204},{16,80},{20,212},{24,88},{28,220},{... | collective-permute-start | bytes 1572872 | tf_op jit(solution)/shard_map/ppermute | solution.py:424
  65.0 11.0 %copy-start.13 = (f32[8,16,512]{2,1,0:T(8,128)}, f32[8,16,512]{2,1,0:T(8,128)S(1)}, u32[]{:S(2)}) copy-start(f32[8,16,512]{2,1,0:T(8,128)S(1)} %collective-permute-done.8.refs_6_) | copy-start | bytes 786436
  65.0 9.5 %collective-permute-start.9 = (f32[8,16,512]{2,1,0:T(8,128)S(1)}, f32[8,16,512]{2,1,0:T(8,128)S(1)}, u32[]{:S(2)}, u32[]{:S(2)}) collective-permute-start(f32[8,16,512]{2,1,0:T(8,128)S(1)} %collective-permute-done.8.refs_6_), channel_id=1, source_target_pairs={{0,56},{4,12},{8,0},{12,20},{16,8},{20,28},{24,16},{28,36},{32,24}... | collective-permute-start | bytes 786440 | tf_op jit(solution)/shard_map/ppermute | solution.py:426
  65.2 10.0 %collective-permute-start.6 = (f32[8,16,512]{2,1,0:T(8,128)}, f32[8,16,512]{2,1,0:T(8,128)S(1)}, u32[]{:S(2)}, u32[]{:S(2)}) collective-permute-start(f32[8,16,512]{2,1,0:T(8,128)} %collective-permute-done.5.refs_3_), channel_id=1, source_target_pairs={{0,8},{4,60},{8,16},{12,4},{16,24},{20,12},{24,32},{28,20},{32,40}... | collective-permute-start | bytes 786440 | tf_op jit(solution)/shard_map/ppermute | solution.py:424
  70.3 5.7 %copy-start.8 = (f32[16,16,512]{2,1,0:T(8,128)}, f32[16,16,512]{2,1,0:T(8,128)S(1)}, u32[]{:S(2)}) copy-start(f32[16,16,512]{2,1,0:T(8,128)S(1)} %collective-permute-done.19.refs_11_) | copy-start | bytes 1572868
  74.5 0.7 copy-start.14
  75.2 0.7 copy-start.15
  76.0 0.8 copy-start.9
  82.2 23.7 %collective-permute-start.20 = (f32[24,32,512]{2,1,0:T(8,128)}, f32[24,32,512]{2,1,0:T(8,128)S(1)}, u32[]{:S(2)}, u32[]{:S(2)}) collective-permute-start(f32[24,32,512]{2,1,0:T(8,128)} %get-tuple-element.27), channel_id=1, source_target_pairs={{0,4},{4,0},{8,12},{12,8},{16,20},{20,16},{24,28},{28,24},{32,36},... | collective-permute-start | bytes 4718600 | tf_op jit(solution)/shard_map/ppermute | solution.py:461
  95.6 11.4 %copy-start.3 = (f32[24,32,512]{2,1,0:T(8,128)S(1)}, f32[24,32,512]{2,1,0:T(8,128)}, u32[]{:S(2)}) copy-start(f32[24,32,512]{2,1,0:T(8,128)} %get-tuple-element.26) | copy-start | bytes 4718596
  105.9 1.2 copy-start.4
  108.9 31.5 %copy-start.1 = (f32[24,32,512]{2,1,0:T(8,128)}, f32[24,32,512]{2,1,0:T(8,128)S(1)}, u32[]{:S(2)}) copy-start(f32[24,32,512]{2,1,0:T(8,128)S(1)} %broadcast_select_fusion.p0) | copy-start | bytes 4718596
  108.9 31.5 %collective-permute-start.21 = (f32[24,32,512]{2,1,0:T(8,128)S(1)}, f32[24,32,512]{2,1,0:T(8,128)S(1)}, u32[]{:S(2)}, u32[]{:S(2)}) collective-permute-start(f32[24,32,512]{2,1,0:T(8,128)S(1)} %broadcast_select_fusion.p0), channel_id=1, source_target_pairs={{0,1},{1,2},{2,3},{3,0},{4,7},{5,4},{6,5},{7,6},{8,9},{9,10},{10,1... | collective-permute-start | bytes 4718600 | tf_op jit(solution)/shard_map/ppermute | solution.py:464
  129.7 16.6 %copy-start.16 = (s32[20,2]{0,1:T(2,128)S(1)}, s32[20,2]{0,1:T(2,128)}, u32[]{:S(2)}) copy-start(s32[20,2]{0,1:T(2,128)} %param.13) | copy-start | bytes 484
  140.4 36.3 %collective-permute-start.22 = (f32[24,32,512]{2,1,0:T(8,128)S(1)}, f32[24,32,512]{2,1,0:T(8,128)}, u32[]{:S(2)}, u32[]{:S(2)}) collective-permute-start(f32[24,32,512]{2,1,0:T(8,128)S(1)} %broadcast_select_fusion.p0), channel_id=1, source_target_pairs={{0,3},{1,0},{2,1},{3,2},{4,5},{5,6},{6,7},{7,4},{8,11},{9,8},{10,9... | collective-permute-start | bytes 4718600 | tf_op jit(solution)/shard_map/ppermute | solution.py:465
  140.5 11.0 %copy-start.2 = (f32[24,32,512]{2,1,0:T(8,128)}, f32[24,32,512]{2,1,0:T(8,128)S(1)}, u32[]{:S(2)}) copy-start(f32[24,32,512]{2,1,0:T(8,128)S(1)} %collective-permute-done.21.p1) | copy-start | bytes 4718596
  140.5 36.3 %collective-permute-start.23 = (f32[24,32,512]{2,1,0:T(8,128)S(1)}, f32[24,32,512]{2,1,0:T(8,128)}, u32[]{:S(2)}, u32[]{:S(2)}) collective-permute-start(f32[24,32,512]{2,1,0:T(8,128)S(1)} %collective-permute-done.21.p1), channel_id=1, source_target_pairs={{0,1},{1,2},{2,3},{3,0},{4,7},{5,4},{6,5},{7,6},{8,9},{9,10},{10,1... | collective-permute-start | bytes 4718600 | tf_op jit(solution)/shard_map/ppermute | solution.py:466
Sparse Core Ops, SparseCore 0:
  10.8 152.5 all-gather.1
